TPU v7x, 32 devices: a whole 2x2x4 slice. The times are simulated.
32 devices in a mesh: gx: 4 (over y, x), yz: 8 (over z, core).
Axes of the slice: x: 2, y: 2, z: 4, core: 2. Of those that a mesh axis runs over, the one named last changes fastest.
Arguments:
- potential: float32 [32, 64, 2048], P('gx', 'yz'), may hold values from -96 to 96
- gal_cells: int32 [4, 8, 8, 128], P('gx', 'yz'), may hold values from 0 to 63
- gal_z: int32 [4, 8, 8, 128], P('gx', 'yz'), may hold values from 0 to 2047
- gal_bins: int32 [4, 8, 8, 128], P('gx', 'yz'), may hold values from 0 to 7
- gal_counts: int32 [4, 8, 8], P('gx', 'yz'), may hold values from 1 to 128, as said below
Outputs:
- tidal: float32 [6, 4, 8, 1024], P(None, 'gx', 'yz')
Inputs may be any that keep to these rules, and one draw needn't show every extreme that they name: For each band g, one tile d receives 128 live slots from every home device; the live slots are the first gal_counts ones.
All inputs are finite; a program needn't handle non-finite values.
Results may differ from a plain program's by a relative error of at most 0.00002.
Values sent between devices are 32-bit elements; how exact they have to be, the bound alone decides.
No kernel may reach another device: no remote copies, remote signals or barrier semaphores. Data moves between devices by JAX's collectives and lax.ppermute only.
A program may use at most 192 MiB of HBM per device.

v0:
```python
import jax
import jax.numpy as jnp
from jax import lax
from jax.sharding import PartitionSpec as P

HALO = 6
BINS = 8


def padded_2(shard, sides, width):
    for axis, dim in sides:
        size, length = (lax.axis_size(axis), shard.shape[dim])
        up = [(i, (i + 1) % size) for i in range(size - 1)]
        down = [(j, i) for i, j in up]
        last = lax.slice_in_dim(shard, length - width, length, axis=dim)
        initial = lax.slice_in_dim(shard, 0, width, axis=dim)
        before = lax.ppermute(last, axis, up)
        after = lax.ppermute(initial, axis, down)
        shard = jnp.concatenate([before, shard, after], axis=dim)
    return shard


def kernels():
    offsets = jnp.arange(-HALO, HALO + 1).astype(jnp.float32)
    sigma_cells = HALO / 3.0
    smooth_w = jnp.exp(-offsets * offsets / (2.0 * sigma_cells * sigma_cells))
    smooth_w = smooth_w / jnp.sum(smooth_w)
    first_w = offsets / (sigma_cells * sigma_cells) * smooth_w
    second_w = (offsets * offsets / sigma_cells**4 - 1.0 / (sigma_cells * sigma_cells)) * smooth_w
    return (smooth_w, first_w, second_w)


def sweep_axis(padded, weights, axis):
    length = padded.shape[axis] - 2 * HALO
    summed = weights[0] * lax.slice_in_dim(padded, 0, length, axis=axis)
    for k in range(1, 2 * HALO + 1):
        summed = summed + weights[k] * lax.slice_in_dim(padded, k, k + length, axis=axis)
    return summed


def tensor_fields(along_x, weights):
    x_smooth, x_first, x_second = along_x
    smooth_w, first_w, second_w = weights
    plans = [
        (x_second, smooth_w, smooth_w),
        (x_smooth, second_w, smooth_w),
        (x_smooth, smooth_w, second_w),
        (x_first, first_w, smooth_w),
        (x_first, smooth_w, first_w),
        (x_smooth, first_w, first_w),
    ]
    results = []
    for field, y_w, z_w in plans:
        in_y = sweep_axis(field, y_w, 1)
        wrapped = jnp.concatenate([in_y[:, :, -HALO:], in_y, in_y[:, :, :HALO]], axis=2)
        results.append(sweep_axis(wrapped, z_w, 2))
    return jnp.stack(results)


def look_up(flat_tensor, z_depth, slot_cells, slot_zeds, slot_bins):
    scale = (HALO / 3.0) ** 2
    here_cell = slot_cells * z_depth + slot_zeds
    next_cell = slot_cells * z_depth + (slot_zeds + 1) % z_depth
    here_value = jnp.take(flat_tensor, here_cell.reshape(-1), axis=1).reshape(
        (6,) + slot_cells.shape
    )
    next_value = jnp.take(flat_tensor, next_cell.reshape(-1), axis=1).reshape(
        (6,) + slot_cells.shape
    )
    weight = (slot_bins.astype(jnp.float32) + 0.5) / BINS
    return ((1.0 - weight) * here_value + weight * next_value) * scale


def build_tensor(potential, weights):
    padded = padded_2(potential, (("gx", 0), ("yz", 1)), HALO)
    along_x = [sweep_axis(padded, w, 0) for w in weights]
    components = tensor_fields(along_x, weights)
    return components.reshape(6, -1)


def body(potential, gal_cells, gal_z, gal_bins, gal_counts):
    weights = kernels()
    z_depth = potential.shape[2]
    tiles = gal_cells.shape[2]
    slots = gal_cells.shape[3]
    slot_cells = gal_cells.reshape(tiles, slots)
    slot_zeds = gal_z.reshape(tiles, slots)
    slot_bins = gal_bins.reshape(tiles, slots)
    flat_tensor = build_tensor(potential, weights)
    served = look_up(
        flat_tensor,
        z_depth,
        lax.all_to_all(slot_cells, "yz", split_axis=0, concat_axis=0, tiled=True),
        lax.all_to_all(slot_zeds, "yz", split_axis=0, concat_axis=0, tiled=True),
        lax.all_to_all(slot_bins, "yz", split_axis=0, concat_axis=0, tiled=True),
    )
    returned = lax.all_to_all(served, "yz", split_axis=1, concat_axis=1, tiled=True)
    slot_index = lax.broadcasted_iota(jnp.int32, (tiles, slots), 1)
    live = slot_index < gal_counts.reshape(tiles, 1)
    tidal = jnp.where(live[None], returned, jnp.float32(0.0))
    return tidal.reshape(6, 1, 1, tiles * slots)


def solution(mesh):
    return jax.shard_map(
        body,
        mesh=mesh,
        in_specs=(
            P("gx", "yz", None),
            P("gx", "yz", None, None),
            P("gx", "yz", None, None),
            P("gx", "yz", None, None),
            P("gx", "yz", None),
        ),
        out_specs=P(None, "gx", "yz", None),
        check_vma=False,
    )
```

profile of v0, /device:TPU:0, one launch (start us, length us, event | category | flops | bytes accessed | tf_op | source)
XLA Modules:
  0.0 297.3 jit_solution(13801150801034493968)
XLA Ops:
  0.0 1.3 copy.27
  1.4 0.1 fusion.228
  1.4 4.9 %collective-permute-start = (f32[6,8,2048]{2,0,1:T(8,128)S(1)}, f32[6,8,2048]{2,0,1:T(8,128)S(1)}, u32[]{:S(2)}, u32[]{:S(2)}) collective-permute-start(f32[6,8,2048]{2,0,1:T(8,128)S(1)} %get-tuple-element.20), channel_id=1, source_target_pairs={{0,8},{8,16},{16,24},{1,9},{9,17},{17,25},{2,10},{10,18},{18,26},{... | collective-permute-start | bytes 1179656 | tf_op jit(solution)/shard_map/ppermute | solution.py:17
  6.4 1.3 collective-permute-start.1
  7.7 4.9 %all-to-all-start = ((s32[8,1,128]{2,1,0:T(1,128)}), s32[8,1,128]{2,1,0:T(1,128)S(1)}, u32[]{:S(2)}, u32[]{:S(2)}) async-start(s32[8,1,128]{2,1,0:T(1,128)} %bitcast.1), calls=%async_computation | async-start | bytes 8192 | tf_op jit(solution)/shard_map/all_to_all | solution.py:95
  12.5 0.6 fusion.220
  13.2 0.7 multiply_multiply_fusion
  13.8 0.7 broadcast_divide_fusion
  14.5 0.7 fusion.230
  15.2 0.7 fusion.229
  15.9 0.7 fusion.231
  16.6 0.9 collective-permute-done
  17.5 13.2 %collective-permute-done.1 = f32[6,8,2048]{2,0,1:T(8,128)S(1)} collective-permute-done((f32[6,8,2048]{2,0,1:T(8,128)S(1)}, f32[6,8,2048]{2,0,1:T(8,128)S(1)}, u32[]{:S(2)}, u32[]{:S(2)}) %collective-permute-start.1) | collective-permute-done | bytes 393248 | tf_op jit(solution)/shard_map/ppermute | solution.py:18
  30.7 0.2 pad_maximum_fusion.1
  30.9 1.7 fusion.221
  32.6 1.4 collective-permute-start.2
  34.0 1.3 collective-permute-start.3
  35.3 7.8 %all-to-all-start.1 = ((s32[8,1,128]{2,1,0:T(1,128)}), s32[8,1,128]{2,1,0:T(1,128)S(1)}, u32[]{:S(2)}, u32[]{:S(2)}) async-start(s32[8,1,128]{2,1,0:T(1,128)} %bitcast.3), calls=%async_computation.1 | async-start | bytes 8192 | tf_op jit(solution)/shard_map/all_to_all | solution.py:93
  43.1 13.1 %all-to-all-done.1 = s32[8,1,128]{2,1,0:T(1,128)S(1)} async-done(((s32[8,1,128]{2,1,0:T(1,128)}), s32[8,1,128]{2,1,0:T(1,128)S(1)}, u32[]{:S(2)}, u32[]{:S(2)}) %all-to-all-start.1) | async-done | bytes 4128 | tf_op jit(solution)/shard_map/all_to_all | solution.py:93
  56.2 3.3 %all-to-all-start.2 = ((s32[8,1,128]{2,1,0:T(1,128)}), s32[8,1,128]{2,1,0:T(1,128)S(1)}, u32[]{:S(2)}, u32[]{:S(2)}) async-start(s32[8,1,128]{2,1,0:T(1,128)} %bitcast.5), calls=%async_computation.2 | async-start | bytes 8192 | tf_op jit(solution)/shard_map/all_to_all | solution.py:94
  59.5 5.4 %all-to-all-done.2 = s32[8,1,128]{2,1,0:T(1,128)S(1)} async-done(((s32[8,1,128]{2,1,0:T(1,128)}), s32[8,1,128]{2,1,0:T(1,128)S(1)}, u32[]{:S(2)}, u32[]{:S(2)}) %all-to-all-start.2) | async-done | bytes 4128 | tf_op jit(solution)/shard_map/all_to_all | solution.py:94
  65.0 1.7 pad_maximum_fusion
  66.8 10.2 %multiply_add_fusion.1 = f32[8,20,2048]{2,0,1:T(8,128)S(1)} fusion(f32[20,20,2048]{2,0,1:T(8,128)S(1)} %pad_maximum_fusion, f32[]{:T(128)} %bitcast.32, f32[]{:T(128)} %bitcast.31, f32[]{:T(128)} %bitcast.30, f32[]{:T(128)} %bitcast.29, f32[]{:T(128)} %bitcast.28, f32[]{:T(128)} %bitcast.27, f32[]{:T(128)} %bitcast.26, f32[]{:T(128)} %bitcast.25, ...), kind=kLoop, calls=%fused_computation.65 | loop fusion | flops 8192000 | bytes 18350132 | tf_op jit(solution)/shard_map/add | solution.py:37
  76.9 10.3 %multiply_add_fusion = f32[8,20,2048]{2,0,1:T(8,128)S(1)} fusion(f32[20,20,2048]{2,0,1:T(8,128)S(1)} %pad_maximum_fusion, f32[]{:T(128)} %bitcast.45, f32[]{:T(128)} %bitcast.44, f32[]{:T(128)} %bitcast.43, f32[]{:T(128)} %bitcast.42, f32[]{:T(128)} %bitcast.41, f32[]{:T(128)} %bitcast.40, f32[]{:T(128)} %bitcast.39, f32[]{:T(128)} %bitcast.38, f32[]{:T(128)} %bitcast.37, ...), kind=kLoop, calls=%fused_computation.64 | loop fusion | flops 8192000 | bytes 18350132 | tf_op jit(solution)/shard_map/add | solution.py:37
  87.3 8.6 %multiply_add_fusion.4 = f32[8,8,2048]{2,0,1:T(8,128)S(1)} fusion(f32[8,20,2048]{2,0,1:T(8,128)S(1)} %multiply_add_fusion, f32[]{:T(128)} %bitcast.32, f32[]{:T(128)} %bitcast.31, f32[]{:T(128)} %bitcast.30, f32[]{:T(128)} %bitcast.29, f32[]{:T(128)} %bitcast.28, f32[]{:T(128)} %bitcast.27, f32[]{:T(128)} %bitcast.26, f32[]{:T(128)} %bitcast.25, ...), kind=kLoop, calls=%fused_computation.345 | loop fusion | flops 3276800 | bytes 7340084 | tf_op jit(solution)/shard_map/add | solution.py:37
  95.9 8.7 %multiply_add_fusion.5 = f32[8,8,2048]{2,0,1:T(8,128)S(1)} fusion(f32[8,20,2048]{2,0,1:T(8,128)S(1)} %multiply_add_fusion, f32[]{:T(128)} %bitcast.45, f32[]{:T(128)} %bitcast.44, f32[]{:T(128)} %bitcast.43, f32[]{:T(128)} %bitcast.42, f32[]{:T(128)} %bitcast.41, f32[]{:T(128)} %bitcast.40, f32[]{:T(128)} %bitcast.39, f32[]{:T(128)} %bitcast.38, ...), kind=kLoop, calls=%fused_computation.346 | loop fusion | flops 3276800 | bytes 7340084 | tf_op jit(solution)/shard_map/add | solution.py:37
  104.6 8.7 %multiply_add_fusion.3 = f32[8,8,2048]{2,0,1:T(8,128)S(1)} fusion(f32[8,20,2048]{2,0,1:T(8,128)S(1)} %multiply_add_fusion.1, f32[]{:T(128)} %bitcast.45, f32[]{:T(128)} %bitcast.44, f32[]{:T(128)} %bitcast.43, f32[]{:T(128)} %bitcast.42, f32[]{:T(128)} %bitcast.41, f32[]{:T(128)} %bitcast.40, f32[]{:T(128)} %bitcast.39, f32[]{:T(128)} %bitcast.38, ...), kind=kLoop, calls=%fused_computation.344 | loop fusion | flops 3276800 | bytes 7340084 | tf_op jit(solution)/shard_map/add | solution.py:37
  113.3 8.6 %multiply_add_fusion.6 = f32[8,8,2048]{2,0,1:T(8,128)S(1)} fusion(f32[8,20,2048]{2,0,1:T(8,128)S(1)} %multiply_add_fusion.1, f32[]{:T(128)} %bitcast.32, f32[]{:T(128)} %bitcast.31, f32[]{:T(128)} %bitcast.30, f32[]{:T(128)} %bitcast.29, f32[]{:T(128)} %bitcast.28, f32[]{:T(128)} %bitcast.27, f32[]{:T(128)} %bitcast.26, f32[]{:T(128)} %bitcast.25, ...), kind=kLoop, calls=%fused_computation.347 | loop fusion | flops 3276800 | bytes 7340084 | tf_op jit(solution)/shard_map/add | solution.py:37
  121.9 8.3 %multiply_add_fusion.7 = f32[8,8,2048]{2,0,1:T(8,128)S(1)} fusion(f32[8,20,2048]{2,0,1:T(8,128)S(1)} %multiply_add_fusion.1, f32[]{:T(128)} %bitcast.20, f32[]{:T(128)} %bitcast.19, f32[]{:T(128)} %bitcast.18, f32[]{:T(128)} %bitcast.17, f32[]{:T(128)} %bitcast.16, f32[]{:T(128)} %bitcast.15, f32[]{:T(128)} %bitcast.14, f32[]{:T(128)} %bitcast.13, ...), kind=kLoop, calls=%fused_computation.348 | loop fusion | flops 3276800 | bytes 7340084 | tf_op jit(solution)/shard_map/add | solution.py:37
  130.3 10.1 %multiply_add_fusion.2 = f32[8,20,2048]{2,0,1:T(8,128)S(1)} fusion(f32[20,20,2048]{2,0,1:T(8,128)S(1)} %pad_maximum_fusion, f32[]{:T(128)} %bitcast.20, f32[]{:T(128)} %bitcast.19, f32[]{:T(128)} %bitcast.18, f32[]{:T(128)} %bitcast.17, f32[]{:T(128)} %bitcast.16, f32[]{:T(128)} %bitcast.15, f32[]{:T(128)} %bitcast.14, f32[]{:T(128)} %bitcast.13, ...), kind=kLoop, calls=%fused_computation.66 | loop fusion | flops 8192000 | bytes 18350132 | tf_op jit(solution)/shard_map/add | solution.py:37
  140.4 0.1 fusion.222
  140.5 10.1 %fusion.3 = f32[8,8,2048]{2,0,1:T(8,128)S(1)} fusion(f32[8,8,6]{2,0,1:T(8,128)S(1)} %get-tuple-element.9, f32[8,8,6]{2,0,1:T(8,128)S(1)} %get-tuple-element.8, f32[8,8,2048]{2,0,1:T(8,128)S(1)} %multiply_add_fusion.3, f32[]{:T(128)} %bitcast.45, f32[]{:T(128)} %bitcast.44, f32[]{:T(128)} %bitcast.43, f32[]{:T(128)} %bitcast.42, f32[]{:T(128)} %bitcast.41, ...), kind=kLoop, calls=%fused_computation.70 | loop fusion | flops 4849664 | bytes 1051700 | tf_op jit(solution)/shard_map/add | solution.py:37
  150.6 1.1 copy.35
  151.7 2.5 stack.26
  154.2 10.1 %fusion.35 = f32[8,8,2048]{2,0,1:T(8,128)S(1)} fusion(f32[8,8,6]{2,0,1:T(8,128)S(1)} %get-tuple-element.11, f32[8,8,6]{2,0,1:T(8,128)S(1)} %get-tuple-element.10, f32[8,8,2048]{2,0,1:T(8,128)S(1)} %multiply_add_fusion.4, f32[]{:T(128)} %bitcast.45, f32[]{:T(128)} %bitcast.44, f32[]{:T(128)} %bitcast.43, f32[]{:T(128)} %bitcast.42, f32[]{:T(128)} %bitcast.41, ...), kind=kLoop, calls=%fused_computation.102 | loop fusion | flops 4849664 | bytes 1051700 | tf_op jit(solution)/shard_map/add | solution.py:37
  164.3 1.1 copy.34
  165.4 1.7 stack.25
  167.1 0.1 fusion.224
  167.1 9.9 %fusion.67 = f32[8,8,2048]{2,0,1:T(8,128)S(1)} fusion(f32[8,8,6]{2,0,1:T(8,128)S(1)} %get-tuple-element.13, f32[8,8,6]{2,0,1:T(8,128)S(1)} %get-tuple-element.12, f32[8,8,2048]{2,0,1:T(8,128)S(1)} %multiply_add_fusion.5, f32[]{:T(128)} %bitcast.32, f32[]{:T(128)} %bitcast.31, f32[]{:T(128)} %bitcast.30, f32[]{:T(128)} %bitcast.29, f32[]{:T(128)} %bitcast.28, ...), kind=kLoop, calls=%fused_computation.134 | loop fusion | flops 4849664 | bytes 1051700 | tf_op jit(solution)/shard_map/add | solution.py:37
  177.1 1.1 copy.33
  178.2 1.7 stack.24
  179.9 9.7 %fusion.99 = f32[8,8,2048]{2,0,1:T(8,128)S(1)} fusion(f32[8,8,6]{2,0,1:T(8,128)S(1)} %get-tuple-element.15, f32[8,8,6]{2,0,1:T(8,128)S(1)} %get-tuple-element.14, f32[8,8,2048]{2,0,1:T(8,128)S(1)} %multiply_add_fusion.6, f32[]{:T(128)} %bitcast.20, f32[]{:T(128)} %bitcast.19, f32[]{:T(128)} %bitcast.18, f32[]{:T(128)} %bitcast.17, f32[]{:T(128)} %bitcast.16, ...), kind=kLoop, calls=%fused_computation.166 | loop fusion | flops 4849664 | bytes 1051700 | tf_op jit(solution)/shard_map/add | solution.py:37
  189.6 1.1 copy.32
  190.7 1.7 stack.23
  192.5 10.1 %fusion.131 = f32[8,8,2048]{2,0,1:T(8,128)S(1)} fusion(f32[8,8,6]{2,0,1:T(8,128)S(1)} %get-tuple-element.17, f32[8,8,6]{2,0,1:T(8,128)S(1)} %get-tuple-element.16, f32[8,8,2048]{2,0,1:T(8,128)S(1)} %multiply_add_fusion.7, f32[]{:T(128)} %bitcast.32, f32[]{:T(128)} %bitcast.31, f32[]{:T(128)} %bitcast.30, f32[]{:T(128)} %bitcast.29, f32[]{:T(128)} %bitcast.28, ...), kind=kLoop, calls=%fused_computation.198 | loop fusion | flops 4849664 | bytes 1051700 | tf_op jit(solution)/shard_map/add | solution.py:37
  202.6 1.1 copy.31
  203.7 1.7 stack.22
  205.4 8.6 %fusion.204 = f32[8,8,2048]{2,0,1:T(8,128)S(1)} fusion(f32[8,20,2048]{2,0,1:T(8,128)S(1)} %multiply_add_fusion.2, f32[]{:T(128)} %bitcast.32, f32[]{:T(128)} %bitcast.31, f32[]{:T(128)} %bitcast.30, f32[]{:T(128)} %bitcast.29, f32[]{:T(128)} %bitcast.28, f32[]{:T(128)} %bitcast.27, f32[]{:T(128)} %bitcast.26, f32[]{:T(128)} %bitcast.25, f32[]{:T(128)} %bitcast.24, ...), kind=kLoop, calls=%fused_computation.320 | loop fusion | flops 3276800 | bytes 7340084 | tf_op jit(solution)/shard_map/add | solution.py:37
  213.9 0.1 fusion.227
  214.0 9.9 %fusion.163 = f32[8,8,2048]{2,0,1:T(8,128)S(1)} fusion(f32[8,8,6]{2,0,1:T(8,128)S(1)} %get-tuple-element.19, f32[8,8,6]{2,0,1:T(8,128)S(1)} %get-tuple-element.18, f32[8,8,2048]{2,0,1:T(8,128)S(1)} %fusion.204, f32[]{:T(128)} %bitcast.32, f32[]{:T(128)} %bitcast.31, f32[]{:T(128)} %bitcast.30, f32[]{:T(128)} %bitcast.29, f32[]{:T(128)} %bitcast.28, ...), kind=kLoop, calls=%fused_computation.230 | loop fusion | flops 4849664 | bytes 1051700 | tf_op jit(solution)/shard_map/add | solution.py:37
  224.0 1.1 copy.30
  225.1 1.7 stack.21
  226.7 8.1 %stack.27 = f32[6,131072]{1,0:T(8,128)} concatenate(f32[1,131072]{1,0:T(1,128)S(1)} %stack.21, f32[1,131072]{1,0:T(1,128)S(1)} %stack.22, f32[1,131072]{1,0:T(1,128)S(1)} %stack.23, f32[1,131072]{1,0:T(1,128)S(1)} %stack.24, f32[1,131072]{1,0:T(1,128)S(1)} %stack.25, f32[1,131072]{1,0:T(1,128)S(1)} %copy-done), dimensions={0} | concatenate | bytes 6291456 | tf_op jit(solution)/shard_map/stack | solution.py:57
  234.9 30.2 %copy.36 = f32[6,131072]{0,1:T(8,128)} copy(f32[6,131072]{1,0:T(8,128)} %stack.27) | data formatting | bytes 6291456 | tf_op jit(solution)/shard_map/stack | solution.py:57
  265.1 10.6 %gather_fusion = f32[1024,6]{1,0:T(8,128)S(1)} fusion(f32[6,131072]{0,1:T(8,128)} %copy.36, s32[1024]{0:T(1024)S(1)} %get-tuple-element.24), kind=kCustom, calls=%fused_computation.clone | custom fusion | bytes 53248 | tf_op jit(solution)/shard_map/jit(_take)/gather | solution.py:64
  275.6 0.2 broadcast_select_fusion.1
  275.9 0.2 copy.37
  276.1 10.5 %gather_fusion.1 = f32[1024,6]{1,0:T(8,128)S(1)} fusion(f32[6,131072]{0,1:T(8,128)} %copy.36, s32[1024]{0:T(1024)S(1)} %get-tuple-element.25), kind=kCustom, calls=%fused_computation.1.clone | custom fusion | bytes 53248 | tf_op jit(solution)/shard_map/jit(_take)/gather | solution.py:67
  286.6 0.2 broadcast_select_fusion
  286.8 0.2 copy.39
  287.0 0.6 add_multiply_fusion
  287.6 3.3 %all-to-all-start.3 = ((f32[6,8,128]{2,0,1:T(8,128)}), f32[6,8,128]{2,0,1:T(8,128)S(1)}, u32[]{:S(2)}, u32[]{:S(2)}) async-start(f32[6,8,128]{2,0,1:T(8,128)} %add_multiply_fusion), calls=%async_computation.3 | async-start | bytes 65536 | tf_op jit(solution)/shard_map/all_to_all | solution.py:97
  291.0 5.6 %all-to-all-done.3 = f32[6,8,128]{2,0,1:T(8,128)S(1)} async-done(((f32[6,8,128]{2,0,1:T(8,128)}), f32[6,8,128]{2,0,1:T(8,128)S(1)}, u32[]{:S(2)}, u32[]{:S(2)}) %all-to-all-start.3) | async-done | bytes 24608 | tf_op jit(solution)/shard_map/all_to_all | solution.py:97
  296.6 0.6 copy.40
  (17 shorter events, 0.4 us)
Async XLA Ops:
  1.4 16.0 %collective-permute-start = (f32[6,8,2048]{2,0,1:T(8,128)S(1)}, f32[6,8,2048]{2,0,1:T(8,128)S(1)}, u32[]{:S(2)}, u32[]{:S(2)}) collective-permute-start(f32[6,8,2048]{2,0,1:T(8,128)S(1)} %get-tuple-element.20), channel_id=1, source_target_pairs={{0,8},{8,16},{16,24},{1,9},{9,17},{17,25},{2,10},{10,18},{18,26},{... | collective-permute-start | bytes 1179656 | tf_op jit(solution)/shard_map/ppermute | solution.py:17
  6.4 24.3 %collective-permute-start.1 = (f32[6,8,2048]{2,0,1:T(8,128)S(1)}, f32[6,8,2048]{2,0,1:T(8,128)S(1)}, u32[]{:S(2)}, u32[]{:S(2)}) collective-permute-start(f32[6,8,2048]{2,0,1:T(8,128)S(1)} %get-tuple-element.21), channel_id=1, source_target_pairs={{8,0},{16,8},{24,16},{9,1},{17,9},{25,17},{10,2},{18,10},{26,18},{... | collective-permute-start | bytes 1179656 | tf_op jit(solution)/shard_map/ppermute | solution.py:18
  7.7 27.6 %all-to-all-start = ((s32[8,1,128]{2,1,0:T(1,128)}), s32[8,1,128]{2,1,0:T(1,128)S(1)}, u32[]{:S(2)}, u32[]{:S(2)}) async-start(s32[8,1,128]{2,1,0:T(1,128)} %bitcast.1), calls=%async_computation | async-start | bytes 8192 | tf_op jit(solution)/shard_map/all_to_all | solution.py:95
  32.6 32.4 %collective-permute-start.2 = (f32[20,6,2048]{2,0,1:T(8,128)}, f32[20,6,2048]{2,0,1:T(8,128)S(1)}, u32[]{:S(2)}, u32[]{:S(2)}) collective-permute-start(f32[20,6,2048]{2,0,1:T(8,128)} %get-tuple-element.6), channel_id=1, source_target_pairs={{0,1},{1,2},{2,3},{3,4},{4,5},{5,6},{6,7},{8,9},{9,10},{10,11},{11... | collective-permute-start | bytes 2949128 | tf_op jit(solution)/shard_map/ppermute | solution.py:17
  34.0 31.0 %collective-permute-start.3 = (f32[20,6,2048]{2,0,1:T(8,128)}, f32[20,6,2048]{2,0,1:T(8,128)}, u32[]{:S(2)}, u32[]{:S(2)}) collective-permute-start(f32[20,6,2048]{2,0,1:T(8,128)} %get-tuple-element.7), channel_id=1, source_target_pairs={{1,0},{2,1},{3,2},{4,3},{5,4},{6,5},{7,6},{9,8},{10,9},{11,10},{12... | collective-permute-start | bytes 2949128 | tf_op jit(solution)/shard_map/ppermute | solution.py:18
  35.3 20.9 %all-to-all-start.1 = ((s32[8,1,128]{2,1,0:T(1,128)}), s32[8,1,128]{2,1,0:T(1,128)S(1)}, u32[]{:S(2)}, u32[]{:S(2)}) async-start(s32[8,1,128]{2,1,0:T(1,128)} %bitcast.3), calls=%async_computation.1 | async-start | bytes 8192 | tf_op jit(solution)/shard_map/all_to_all | solution.py:93
  56.2 8.8 %all-to-all-start.2 = ((s32[8,1,128]{2,1,0:T(1,128)}), s32[8,1,128]{2,1,0:T(1,128)S(1)}, u32[]{:S(2)}, u32[]{:S(2)}) async-start(s32[8,1,128]{2,1,0:T(1,128)} %bitcast.5), calls=%async_computation.2 | async-start | bytes 8192 | tf_op jit(solution)/shard_map/all_to_all | solution.py:94
  223.9 2.8 copy-start
  275.9 15.1 %copy-start.1 = (s32[1,1,8]{2,1,0:T(1,128)S(1)}, s32[1,1,8]{2,1,0:T(1,128)}, u32[]{:S(2)}) copy-start(s32[1,1,8]{2,1,0:T(1,128)} %param.11) | copy-start | bytes 100
  287.6 9.0 %all-to-all-start.3 = ((f32[6,8,128]{2,0,1:T(8,128)}), f32[6,8,128]{2,0,1:T(8,128)S(1)}, u32[]{:S(2)}, u32[]{:S(2)}) async-start(f32[6,8,128]{2,0,1:T(8,128)} %add_multiply_fusion), calls=%async_computation.3 | async-start | bytes 65536 | tf_op jit(solution)/shard_map/all_to_all | solution.py:97
where the time goes:
time: 300 us; the launch traced here: 297 us
  other arithmetic  147 us (49%)
  local copies, waits for them, and re-layouts  83.5 us (28%)
  waiting for transfers between devices  38.2 us (13%)
  starting transfers between devices  28.2 us (9%)
    add x15, other arithmetic, sweep_axis(): summed + weights[k] * lax.slice_in_dim(padded, k, k + length, axis=axis)  142 us
    another operation x8, local copies, waits for them, and re-layouts, tensor_fields(): return jnp.stack(results)  49.1 us
    ppermute x2, waiting for transfers between devices, padded_2(): after = lax.ppermute(initial, axis, down)  13.2 us
    all_to_all x1, waiting for transfers between devices, body(): lax.all_to_all(slot_cells, 'yz', split_axis=0, concat_axis=0, tiled=True)  13.1 us
    gather x1, local copies, waits for them, and re-layouts, look_up(): jnp.take(flat_tensor, here_cell.reshape(-1), axis=1)  10.6 us
    gather x1, local copies, waits for them, and re-layouts, look_up(): jnp.take(flat_tensor, next_cell.reshape(-1), axis=1)  10.5 us
    all_to_all x1, starting transfers between devices, body(): lax.all_to_all(slot_cells, 'yz', split_axis=0, concat_axis=0, tiled=True)  7.8 us
    add x6, local copies, waits for them, and re-layouts, sweep_axis(): summed + weights[k] * lax.slice_in_dim(padded, k, k + length, axis=axis)  6.65 us
  transfers between devices with their start and end apart: 8, of which 5 were waited for; matrix products, arithmetic and copies ran while one was open for 2% of the time, Pallas kernels for 0%

commit v1 on v0

v1 whole, which is shorter than its diff:
```python
import functools

import jax
import jax.numpy as jnp
import numpy as np
from jax import lax
from jax.experimental import pallas as pl
from jax.experimental.pallas import tpu as pltpu
from jax.sharding import PartitionSpec as P

HALO = 6
BINS = 8
LANES = 128
SUBS = 8
PARTS = 8
ALONG_X = (2, 0, 0, 1, 1, 0)
ALONG_Y = (0, 2, 0, 1, 0, 1)
ALONG_Z = (0, 0, 2, 0, 1, 1)


def taps():
    offsets = np.arange(-HALO, HALO + 1).astype(np.float32)
    sigma = np.float32(HALO / 3.0)
    smooth = np.exp(-offsets * offsets / (2 * sigma * sigma)).astype(np.float32)
    smooth = smooth / np.sum(smooth, dtype=np.float32)
    first = offsets / (sigma * sigma) * smooth
    second = (offsets * offsets / sigma**4 - 1 / (sigma * sigma)) * smooth
    return np.stack([smooth, first, second]).astype(np.float32)


def z_taps(rows):
    along = taps()
    table = np.zeros((2 * HALO + 1, 2, PARTS, rows), np.float32)
    for a, f in enumerate(ALONG_Z):
        table[:, :, a, :] = along[f][:, None, None]
    return table.reshape(2 * HALO + 1, LANES)


def x_table(planes, rows):
    along = taps()
    scale = np.float32((HALO / 3.0) ** 2)
    table = np.zeros((3 * planes, 2, planes // 2, 2, PARTS, rows), np.float32)
    for at in range(3 * planes):
        for x in range(planes):
            k = x - (at - planes)
            if abs(k) <= HALO:
                for a, f in enumerate(ALONG_X):
                    table[at, :, x // 2, x % 2, a, :] = along[f][k + HALO] * scale
    return table.reshape(3 * planes, SUBS, LANES)


def field_kernel(before, own, after, ztap, xtab, field, table, mid, turn, *, rows, depth):
    along = taps()
    ys = HALO
    per = depth // LANES

    upper = lax.broadcasted_iota(jnp.int32, (SUBS, LANES), 0) >= SUBS // 2
    for b in range(BINS):
        w = np.float32((b + 0.5) / BINS)
        cell_w = jnp.where(upper, w, np.float32(1.0) - w)
        for at in range(xtab.shape[0]):
            table[pl.ds((at * BINS + b) * SUBS, SUBS), :] = xtab[at] * cell_w

    def along_y(block, _):
        z0 = pl.multiple_of(block * LANES, LANES)
        zs = pl.ds(z0, LANES)
        u = [before[y, :, zs] for y in range(HALO)]
        u += [own[y, :, zs] for y in range(rows)]
        u += [after[y, :, zs] for y in range(HALO)]
        for r in range(rows):
            c = u[r + HALO]
            smooth = c * along[0][HALO]
            second = c * along[2][HALO]
            first = None
            for k in range(1, HALO + 1):
                up, down = u[r + HALO + k], u[r + HALO - k]
                both = up + down
                smooth = smooth + both * along[0][HALO + k]
                second = second + both * along[2][HALO + k]
                part = (up - down) * along[1][HALO + k]
                first = part if first is None else first + part
            for f, v in enumerate((smooth, first, second)):
                turn[pl.ds((f * rows + r) * SUBS, SUBS), :] = v
        for pair in range(SUBS // 2):
            tiles = []
            for half in range(2):
                x = 2 * pair + half
                by_filter = [turn[pl.ds(f * rows * SUBS + x, rows, stride=SUBS), :] for f in range(3)]
                tiles += [by_filter[ALONG_Y[a]] for a in range(6)] + [jnp.zeros_like(by_filter[0])] * 2
            flipped = jnp.concatenate(tiles, axis=0).T
            mid[pl.ds((z0 + SUBS) * 4 + pair, LANES, stride=4), :] = flipped
        return 0

    lax.fori_loop(0, per, along_y, 0)
    mid[pl.ds(0, 32), :] = mid[pl.ds(depth * 4, 32), :]
    mid[pl.ds((depth + SUBS) * 4, 32), :] = mid[pl.ds(32, 32), :]

    n = 8
    tap = [jnp.broadcast_to(ztap[k : k + 1, :], (SUBS, LANES)) for k in range(2 * HALO + 1)]

    def along_z(block, _):
        base = pl.multiple_of(block * (n * SUBS), n * SUBS)
        even = [mid[pl.ds(base + 8 + SUBS * j, SUBS), :] for j in range(n + 6)]
        odd = [mid[pl.ds(base + 12 + SUBS * j, SUBS), :] for j in range(n + 5)]
        for j in range(n):
            total = None
            for k in range(-HALO, HALO + 1):
                v = even[j + (k + HALO) // 2] if k % 2 == 0 else odd[j + (k + HALO) // 2]
                part = v * tap[k + HALO]
                total = part if total is None else total + part
            field[pl.ds(base + SUBS * j, SUBS), :] = total
        return 0

    lax.fori_loop(0, depth * 4 // (n * SUBS), along_z, 0)
    field[pl.ds(depth * 4, SUBS), :] = field[pl.ds(0, SUBS), :]


def lookup_kernel(words, place, rows_of, field, table, out, prod, *, bands, planes):
    me = place[0]
    homes = words.shape[0] // bands
    subs = lax.broadcasted_iota(jnp.int32, (SUBS, LANES), 0)

    def one_row(row, _):
        for j in range(LANES):
            word = words[row, j]
            at = (word & 0xFFFF) * 4
            w_at = pl.multiple_of((word >> 16) * SUBS, SUBS)
            prod[pl.ds(j * SUBS, SUBS), :] = field[pl.ds(at, SUBS), :] * table[pl.ds(w_at, SUBS), :]
        groups = []
        for i in range(LANES // SUBS):
            total = prod[pl.ds(i * SUBS * SUBS, SUBS, stride=SUBS), :]
            for s in range(1, SUBS):
                total = total + prod[pl.ds(i * SUBS * SUBS + s, SUBS, stride=SUBS), :]
            groups.append(total)
        flipped = jnp.concatenate(groups, axis=0).T
        mine = rows_of[pl.ds(row, 1), :] == subs
        for a in range(6):
            v = flipped[a * 8 : a * 8 + 8] + flipped[64 + a * 8 : 64 + a * 8 + 8]
            out[row, a, :] = jnp.sum(jnp.where(mine, v, 0.0), axis=0)
        return 0

    for band in range(bands):
        near = jnp.abs(band - me) <= 1

        @pl.when(near)
        def _():
            lax.fori_loop(band * homes, (band + 1) * homes, one_row, 0)

        @pl.when(jnp.logical_not(near))
        def _():
            out[pl.ds(band * homes, homes)] = jnp.zeros((homes, 6, LANES), jnp.float32)


def body(potential, gal_cells, gal_z, gal_bins, gal_counts):
    bands = lax.axis_size("gx")
    homes = lax.axis_size("yz")
    planes, rows, depth = potential.shape
    tiles, slots = gal_cells.shape[2:]
    assert planes == SUBS and rows == SUBS and slots == LANES
    vmem = pl.BlockSpec(memory_space=pltpu.VMEM)
    smem = pl.BlockSpec(memory_space=pltpu.SMEM)

    by_row = potential.transpose(1, 0, 2)
    up = [(i, i + 1) for i in range(homes - 1)]
    down = [(j, i) for i, j in up]
    before = lax.ppermute(by_row[rows - HALO :], "yz", up)
    after = lax.ppermute(by_row[:HALO], "yz", down)

    asked = jnp.concatenate([gal_cells, gal_z, gal_bins], axis=0).reshape(3, tiles, slots).transpose(1, 0, 2)
    asked = jnp.broadcast_to(asked[None], (bands, tiles, 3, slots)).reshape(bands * tiles, 3, slots)
    asked = lax.all_to_all(asked, ("gx", "yz"), split_axis=0, concat_axis=0, tiled=True)

    field, table = pl.pallas_call(
        functools.partial(field_kernel, rows=rows, depth=depth),
        out_shape=(
            jax.ShapeDtypeStruct((depth * 4 + SUBS, LANES), jnp.float32),
            jax.ShapeDtypeStruct((3 * planes * BINS * SUBS, LANES), jnp.float32),
        ),
        in_specs=[vmem] * 5,
        out_specs=(vmem, vmem),
        scratch_shapes=[
            pltpu.VMEM((depth * 4 + 8 * SUBS, LANES), jnp.float32),
            pltpu.VMEM((3 * rows * SUBS, LANES), jnp.float32),
        ],
    )(before, by_row, after, jnp.asarray(z_taps(rows)), jnp.asarray(x_table(planes, rows)))

    me = lax.axis_index("gx")
    band_of = lax.broadcasted_iota(jnp.int32, (bands * homes, slots), 0) // homes
    cells, zeds, bins = asked[:, 0], asked[:, 1], asked[:, 2]
    near = jnp.abs(band_of - me) <= 1
    at = jnp.where(near, (band_of - me + 1) * planes + cells // rows, 0)
    words = zeds + (at * BINS + bins) * 65536
    served = pl.pallas_call(
        functools.partial(lookup_kernel, bands=bands, planes=planes),
        out_shape=jax.ShapeDtypeStruct((bands * homes, 6, slots), jnp.float32),
        in_specs=[smem, smem, vmem, vmem, vmem],
        out_specs=vmem,
        scratch_shapes=[pltpu.VMEM((LANES * SUBS, LANES), jnp.float32)],
    )(words, me.reshape(1), cells % rows, field, table)

    returned = lax.all_to_all(served, ("gx", "yz"), split_axis=0, concat_axis=0, tiled=True)
    total = jnp.sum(returned.reshape(bands, tiles, 6, slots), axis=0)
    slot_index = lax.broadcasted_iota(jnp.int32, (tiles, slots), 1)
    live = slot_index < gal_counts.reshape(tiles, 1)
    tidal = jnp.where(live[None], total.transpose(1, 0, 2), jnp.float32(0.0))
    return tidal.reshape(6, 1, 1, tiles * slots)


def solution(mesh):
    return jax.shard_map(
        body,
        mesh=mesh,
        in_specs=(
            P("gx", "yz", None),
            P("gx", "yz", None, None),
            P("gx", "yz", None, None),
            P("gx", "yz", None, None),
            P("gx", "yz", None),
        ),
        out_specs=P(None, "gx", "yz", None),
        check_vma=False,
    )
```

time: 300 us -> 60.2 us (0.20)
  other arithmetic: 147 us -> 1.52 us
  local copies, waits for them, and re-layouts: 83.5 us -> 3.99 us
  waiting for transfers between devices: 38.2 us -> 10.7 us
  Pallas kernels: 0 us -> 20.8 us
  starting transfers between devices: 28.2 us -> 22.7 us
    add x15 -> x0, other arithmetic: 142 us -> none  [sweep_axis(): summed + weights[k] * lax.slice_in_dim(padded, k, k + length, axis=axis)]
    another operation x8 -> x0, local copies, waits for them, and re-layouts: 49.1 us -> none  [tensor_fields(): return jnp.stack(results)]
    gather x2 -> x0, local copies, waits for them, and re-layouts: 21.1 us -> none  [the longest x1 10.6 us: look_up(): jnp.take(flat_tensor, here_cell.reshape(-1), axis=1)]
    pallas_call x0 -> x2, Pallas kernels: none -> 20.8 us  [the longest x1 11.5 us: body(): pl.pallas_call(functools.partial(field_kernel, rows=rows, depth=depth), o...]
    ppermute x4 -> x2, waiting for transfers between devices: 14.1 us -> 0.25 us  [the longest x1 0.24 us: body(): after = lax.ppermute(by_row[:HALO], 'yz', down)]
    all_to_all x4 -> x2, waiting for transfers between devices: 24.1 us -> 10.5 us  [the longest x1 8.08 us: body(): lax.all_to_all(served, ('gx', 'yz'), split_axis=0, concat_axis=0, tiled=T...]
    add x6 -> x0, local copies, waits for them, and re-layouts: 6.65 us -> none  [sweep_axis(): summed + weights[k] * lax.slice_in_dim(padded, k, k + length, axis=axis)]
    ppermute x4 -> x2, starting transfers between devices: 8.84 us -> 3.47 us  [the longest x1 2.18 us: body(): before = lax.ppermute(by_row[rows - HALO:], 'yz', up)]
  transfers between devices with their start and end apart: 8 -> 4, of which waited for: 5 -> 3; matrix products, arithmetic and copies ran while one was open for 2% -> 4% of each run, Pallas kernels for 0% -> 0%
where the time goes in v1:
time: 60.2 us; the launch traced here: 59.8 us
  starting transfers between devices  22.7 us (38%)
  Pallas kernels  20.8 us (35%)
  waiting for transfers between devices  10.7 us (18%)
  local copies, waits for them, and re-layouts  3.99 us (7%)
  other arithmetic  1.52 us (3%)
    all_to_all x1, starting transfers between devices, body(): lax.all_to_all(served, ('gx', 'yz'), split_axis=0, concat_axis=0, tiled=T...  11.9 us
    pallas_call x1, Pallas kernels, body(): pl.pallas_call(functools.partial(field_kernel, rows=rows, depth=depth), o...  11.5 us
    pallas_call x1, Pallas kernels, body(): pl.pallas_call(functools.partial(lookup_kernel, bands=bands, planes=plane...  9.27 us
    all_to_all x1, waiting for transfers between devices, body(): lax.all_to_all(served, ('gx', 'yz'), split_axis=0, concat_axis=0, tiled=T...  8.08 us
    all_to_all x1, starting transfers between devices, body(): lax.all_to_all(asked, ('gx', 'yz'), split_axis=0, concat_axis=0, tiled=True)  7.33 us
    unnamed x9, local copies, waits for them, and re-layouts  2.61 us
    all_to_all x1, waiting for transfers between devices, body(): lax.all_to_all(asked, ('gx', 'yz'), split_axis=0, concat_axis=0, tiled=True)  2.42 us
    ppermute x1, starting transfers between devices, body(): before = lax.ppermute(by_row[rows - HALO:], 'yz', up)  2.18 us
  transfers between devices with their start and end apart: 4, of which 3 were waited for; matrix products, arithmetic and copies ran while one was open for 4% of the time, Pallas kernels for 0%

profile of v1, /device:TPU:0, one launch (start us, length us, event | category | flops | bytes accessed | tf_op | source)
XLA Modules:
  0.0 59.8 jit_solution(7446832175030093278)
XLA Ops:
  0.0 0.7 %add_bitcast_fusion = s32[8,3,128]{2,0,1:T(8,128)S(1)} fusion(s32[1,1,8,128]{3,2,1,0:T(8,128)} %param.10, s32[1,1,8,128]{3,2,1,0:T(8,128)} %param.9, s32[1,1,8,128]{3,2,1,0:T(8,128)} %param.8), kind=kLoop, calls=%fused_computation.16 | loop fusion | flops 6144 | bytes 24576 | tf_op jit(solution)/shard_map/transpose | solution.py:169
  0.7 0.6 %broadcast_in_dim.22 = s32[4,8,3,128]{3,2,1,0:T(4,128)} broadcast(s32[8,3,128]{2,1,0:T(4,128)S(1)} %copy.14), dimensions={1,2,3} | broadcast | bytes 61440 | tf_op jit(solution)/shard_map/broadcast_in_dim | solution.py:170
  1.4 7.3 %all-to-all-start = ((s32[32,3,128]{2,1,0:T(4,128)}), s32[32,3,128]{2,1,0:T(4,128)S(1)}, u32[]{:S(2)}, u32[]{:S(2)}) async-start(s32[32,3,128]{2,1,0:T(4,128)} %bitcast.3), calls=%async_computation | async-start | bytes 131072 | tf_op jit(solution)/shard_map/all_to_all | solution.py:171
  8.7 1.4 %copy.24 = f32[8,8,2048]{2,0,1:T(8,128)S(1)} copy(f32[8,8,2048]{2,1,0:T(8,128)} %param.7) | data formatting | bytes 1048576 | tf_op args[0]
  10.1 0.0 copy-start
  10.1 0.0 copy-start.3
  10.1 0.1 fusion.8
  10.2 2.2 %collective-permute-start = (f32[6,8,2048]{2,1,0:T(8,128)S(1)}, f32[6,8,2048]{2,1,0:T(8,128)S(1)}, u32[]{:S(2)}, u32[]{:S(2)}) collective-permute-start(f32[6,8,2048]{2,1,0:T(8,128)S(1)} %get-tuple-element.10), channel_id=1, source_target_pairs={{0,1},{1,2},{2,3},{3,4},{4,5},{5,6},{6,7},{8,9},{9,10},{10,11},{11... | collective-permute-start | bytes 1179656 | tf_op jit(solution)/shard_map/ppermute | solution.py:166
  12.3 1.3 %collective-permute-start.1 = (f32[6,8,2048]{2,1,0:T(8,128)S(1)}, f32[6,8,2048]{2,1,0:T(8,128)S(1)}, u32[]{:S(2)}, u32[]{:S(2)}) collective-permute-start(f32[6,8,2048]{2,1,0:T(8,128)S(1)} %get-tuple-element.9), channel_id=1, source_target_pairs={{1,0},{2,1},{3,2},{4,3},{5,4},{6,5},{7,6},{9,8},{10,9},{11,10},{12... | collective-permute-start | bytes 1179656 | tf_op jit(solution)/shard_map/ppermute | solution.py:167
  13.7 2.4 %all-to-all-done = s32[32,3,128]{2,1,0:T(4,128)S(1)} async-done(((s32[32,3,128]{2,1,0:T(4,128)}), s32[32,3,128]{2,1,0:T(4,128)S(1)}, u32[]{:S(2)}, u32[]{:S(2)}) %all-to-all-start) | async-done | bytes 49184 | tf_op jit(solution)/shard_map/all_to_all | solution.py:171
  16.1 0.7 %add_select_fusion = (s32[32,128]{1,0:T(8,128)}, s32[32,128]{1,0:T(8,128)}) fusion(s32[32,128]{1,0:T(8,128)S(1)} %bitcast.27, s32[32,128]{1,0:T(8,128)S(1)} %bitcast.28, s32[32,128]{1,0:T(8,128)S(1)} %bitcast.29, s32[]{:T(128)} %axis_index.15, s32[32]{0:T(128)S(1)} %get-tuple-element.16, s32[32]{0:T(128)S(1)} %get-tuple-element.17, ...), kind=kLoop, calls=%fused_computation.2 | loop fusion | flops 126976 | bytes 82212 | tf_op jit(solution)/shard_map/jit(remainder)/select_n | solution.py:199
  16.8 0.0 collective-permute-done.before
  16.8 0.0 copy-start.1
  16.8 0.2 collective-permute-done.1.after
  17.1 0.0 copy-done
  17.1 0.5 copy-done.1
  17.6 0.0 copy-start.2
  17.6 0.7 %copy-done.2 = f32[6,8,2048]{2,1,0:T(8,128)} copy-done((f32[6,8,2048]{2,1,0:T(8,128)}, f32[6,8,2048]{2,1,0:T(8,128)S(1)}, u32[]{:S(2)}) %copy-start.2) | copy-done | bytes 393240
  18.3 11.5 %shard_map.73 = (f32[8200,128]{1,0:T(8,128)}, f32[1536,128]{1,0:T(8,128)}) custom-call(f32[6,8,2048]{2,1,0:T(8,128)} %copy-done.1, f32[8,8,2048]{2,1,0:T(8,128)} %bitcast.25, f32[6,8,2048]{2,1,0:T(8,128)} %copy-done.2, f32[13,128]{1,0:T(8,128)} %constant.55.clone.ztap, f32[24,8,128]{2,1,0:T(8,128)} %constant.56.clone.xtab), custom_call_target="tpu_custom_call" | custom-call | tf_op jit(solution)/shard_map/pallas_call | solution.py:173
  29.8 9.3 %shard_map.74 = f32[32,6,128]{2,1,0:T(8,128)} custom-call(s32[32,128]{1,0:T(8,128)} %get-tuple-element.15.words, s32[1]{0:T(128)} %bitcast.7.place, s32[32,128]{1,0:T(8,128)} %get-tuple-element.14.rows_of, f32[8200,128]{1,0:T(8,128)} %get-tuple-element.7.field, f32[1536,128]{1,0:T(8,128)} %get-tuple-element.8.table), custom_call_target="tpu_custom_call" | custom-call | tf_op jit(solution)/shard_map/pallas_call | solution.py:193
  39.1 11.9 %all-to-all-start.1 = ((f32[32,6,128]{2,1,0:T(8,128)}), f32[32,6,128]{2,1,0:T(8,128)S(1)}, u32[]{:S(2)}, u32[]{:S(2)}) async-start(f32[32,6,128]{2,1,0:T(8,128)} %shard_map.74), calls=%async_computation.1 | async-start | bytes 262144 | tf_op jit(solution)/shard_map/all_to_all | solution.py:201
  51.0 0.0 copy-done.3
  51.0 0.1 iota_compare_fusion
  51.1 8.1 %all-to-all-done.1 = f32[32,6,128]{2,1,0:T(8,128)S(1)} async-done(((f32[32,6,128]{2,1,0:T(8,128)}), f32[32,6,128]{2,1,0:T(8,128)S(1)}, u32[]{:S(2)}, u32[]{:S(2)}) %all-to-all-start.1) | async-done | bytes 98336 | tf_op jit(solution)/shard_map/all_to_all | solution.py:201
  59.2 0.6 %copy.19 = f32[6,1,1,1024]{3,2,1,0:T(1,128)} copy(f32[6,1,1,1024]{3,0,2,1:T(8,128)S(1)} %select_bitcast_fusion) | data formatting | bytes 49152 | tf_op jit(solution)/shard_map/reshape | solution.py:206
  (6 shorter events, 0.1 us)
Async XLA Ops:
  1.4 14.7 %all-to-all-start = ((s32[32,3,128]{2,1,0:T(4,128)}), s32[32,3,128]{2,1,0:T(4,128)S(1)}, u32[]{:S(2)}, u32[]{:S(2)}) async-start(s32[32,3,128]{2,1,0:T(4,128)} %bitcast.3), calls=%async_computation | async-start | bytes 131072 | tf_op jit(solution)/shard_map/all_to_all | solution.py:171
  10.1 7.0 %copy-start = (f32[8,8,2048]{2,0,1:T(8,128)}, f32[8,8,2048]{2,0,1:T(8,128)S(1)}, u32[]{:S(2)}) copy-start(f32[8,8,2048]{2,0,1:T(8,128)S(1)} %copy.24) | copy-start | bytes 1572868
  10.1 40.9 %copy-start.3 = (s32[1,1,8]{2,1,0:T(1,128)S(1)}, s32[1,1,8]{2,1,0:T(1,128)}, u32[]{:S(2)}) copy-start(s32[1,1,8]{2,1,0:T(1,128)} %param.11) | copy-start | bytes 100
  10.2 6.7 %collective-permute-start = (f32[6,8,2048]{2,1,0:T(8,128)S(1)}, f32[6,8,2048]{2,1,0:T(8,128)S(1)}, u32[]{:S(2)}, u32[]{:S(2)}) collective-permute-start(f32[6,8,2048]{2,1,0:T(8,128)S(1)} %get-tuple-element.10), channel_id=1, source_target_pairs={{0,1},{1,2},{2,3},{3,4},{4,5},{5,6},{6,7},{8,9},{9,10},{10,11},{11... | collective-permute-start | bytes 1179656 | tf_op jit(solution)/shard_map/ppermute | solution.py:166
  12.3 4.7 %collective-permute-start.1 = (f32[6,8,2048]{2,1,0:T(8,128)S(1)}, f32[6,8,2048]{2,1,0:T(8,128)S(1)}, u32[]{:S(2)}, u32[]{:S(2)}) collective-permute-start(f32[6,8,2048]{2,1,0:T(8,128)S(1)} %get-tuple-element.9), channel_id=1, source_target_pairs={{1,0},{2,1},{3,2},{4,3},{5,4},{6,5},{7,6},{9,8},{10,9},{11,10},{12... | collective-permute-start | bytes 1179656 | tf_op jit(solution)/shard_map/ppermute | solution.py:167
  16.8 0.8 %copy-start.1 = (f32[6,8,2048]{2,1,0:T(8,128)}, f32[6,8,2048]{2,1,0:T(8,128)S(1)}, u32[]{:S(2)}) copy-start(f32[6,8,2048]{2,1,0:T(8,128)S(1)} %collective-permute-done.before) | copy-start | bytes 1179652
  17.6 0.7 %copy-start.2 = (f32[6,8,2048]{2,1,0:T(8,128)}, f32[6,8,2048]{2,1,0:T(8,128)S(1)}, u32[]{:S(2)}) copy-start(f32[6,8,2048]{2,1,0:T(8,128)S(1)} %collective-permute-done.1.after) | copy-start | bytes 1179652
  39.1 20.0 %all-to-all-start.1 = ((f32[32,6,128]{2,1,0:T(8,128)}), f32[32,6,128]{2,1,0:T(8,128)S(1)}, u32[]{:S(2)}, u32[]{:S(2)}) async-start(f32[32,6,128]{2,1,0:T(8,128)} %shard_map.74), calls=%async_computation.1 | async-start | bytes 262144 | tf_op jit(solution)/shard_map/all_to_all | solution.py:201

commit v2 on v1

v2 whole, which is shorter than its diff:
```python
import functools

import jax
import jax.numpy as jnp
import numpy as np
from jax import lax
from jax.experimental import pallas as pl
from jax.experimental.pallas import tpu as pltpu
from jax.sharding import PartitionSpec as P


HALO = 6
BINS = 8
LANES = 128
SUBS = 8
PARTS = 8
ALONG_X = (2, 0, 0, 1, 1, 0)
ALONG_Y = (0, 2, 0, 1, 0, 1)
ALONG_Z = (0, 0, 2, 0, 1, 1)


def taps():
    offsets = np.arange(-HALO, HALO + 1).astype(np.float32)
    sigma = np.float32(HALO / 3.0)
    smooth = np.exp(-offsets * offsets / (2 * sigma * sigma)).astype(np.float32)
    smooth = smooth / np.sum(smooth, dtype=np.float32)
    first = offsets / (sigma * sigma) * smooth
    second = (offsets * offsets / sigma**4 - 1 / (sigma * sigma)) * smooth
    return np.stack([smooth, first, second]).astype(np.float32)


def spread(along, values):
    part = lax.broadcasted_iota(jnp.int32, (SUBS, LANES), 1) // SUBS % PARTS
    out = jnp.full((SUBS, LANES), values[along[0]], jnp.float32)
    for a in range(1, len(along)):
        if along[a] != along[0]:
            out = jnp.where(part == a, values[along[a]], out)
    return out


def field_kernel(before, own, after, field, mid, flip, turn, done, sent, *, rows, depth, chunks):
    along = taps()
    blocks = depth // LANES
    odd_sign = spread(ALONG_Z, (1.0, -1.0, 1.0))

    def along_y(block, slot):
        zs = pl.ds(pl.multiple_of(block * LANES, LANES), LANES)
        u = [before[y, :, zs] for y in range(HALO)]
        u += [own[y, :, zs] for y in range(rows)]
        u += [after[y, :, zs] for y in range(HALO)]
        for r in range(rows):
            c = u[r + HALO]
            smooth = c * along[0][HALO]
            second = c * along[2][HALO]
            first = None
            for k in range(1, HALO + 1):
                up, down = u[r + HALO + k], u[r + HALO - k]
                both = up + down
                smooth = smooth + both * along[0][HALO + k]
                second = second + both * along[2][HALO + k]
                part = (up - down) * along[1][HALO + k]
                first = part if first is None else first + part
            for f, v in enumerate((smooth, first, second)):
                turn[slot, pl.ds((f * rows + r) * SUBS, SUBS), :] = v

    def transpose(block, slot):
        base = pl.multiple_of(block * (LANES * 4), LANES * 4) + SUBS * 4
        for pair in range(SUBS // 2):
            tiles = []
            for half in range(2):
                x = 2 * pair + half
                by_filter = [turn[slot, pl.ds(f * rows * SUBS + x, rows, stride=SUBS), :] for f in range(3)]
                tiles += [by_filter[ALONG_Y[a]] for a in range(6)] + [by_filter[0]] * 2
            flipped = jnp.concatenate(tiles, axis=0).T
            mid[pl.ds(base + pair, LANES, stride=4), :] = flipped
            signed = flipped.reshape(LANES // SUBS, SUBS, LANES) * odd_sign
            flip[pl.ds(base + pair, LANES, stride=4), :] = signed.reshape(LANES, LANES)

    along_y(0, 0)

    def two_blocks(i, _):
        along_y(2 * i + 1, 1)
        transpose(2 * i, 0)
        along_y(2 * i + 2, 0)
        transpose(2 * i + 1, 1)
        return 0

    lax.fori_loop(0, blocks // 2 - 1, two_blocks, 0)
    along_y(blocks - 1, 1)
    transpose(blocks - 2, 0)
    transpose(blocks - 1, 1)
    for buf in (mid, flip):
        buf[pl.ds(0, 32), :] = buf[pl.ds(depth * 4, 32), :]
        buf[pl.ds((depth + SUBS) * 4, 32), :] = buf[pl.ds(32, 32), :]

    n = 16
    tap = [spread(ALONG_Z, along[:, k + HALO]) for k in range(HALO + 1)]
    size = depth * 4 // chunks
    steps = size // (n * SUBS)

    def along_z(block, _):
        base = pl.multiple_of(block * (n * SUBS), n * SUBS)
        for j in range(n):
            at = base + SUBS * j + 32
            total = mid[pl.ds(at, SUBS), :] * tap[0]
            for k in range(1, HALO + 1):
                total = total + (mid[pl.ds(at + 4 * k, SUBS), :] + flip[pl.ds(at - 4 * k, SUBS), :]) * tap[k]
            done[pl.ds(base + SUBS * j, SUBS), :] = total
        return 0

    def send(c):
        part = pl.ds(pl.multiple_of(c * size, size), size)
        return pltpu.make_async_copy(done.at[part], field.at[part], sent.at[c])

    wrap = pltpu.make_async_copy(done.at[pl.ds(0, SUBS)], field.at[pl.ds(depth * 4, SUBS)], sent.at[chunks])

    def one_chunk(c, _):
        lax.fori_loop(c * steps, (c + 1) * steps, along_z, 0)
        send(c).start()
        return 0

    lax.fori_loop(0, chunks, one_chunk, 0)
    wrap.start()
    for c in range(chunks):
        send(c).wait()
    wrap.wait()


def fill_table(table, planes):
    along = taps()
    scale = np.float32((HALO / 3.0) ** 2)
    sub = lax.broadcasted_iota(jnp.int32, (SUBS, LANES), 0)
    lane = lax.broadcasted_iota(jnp.int32, (SUBS, LANES), 1)
    upper = sub >= SUBS // 2
    plane = sub % (SUBS // 2) * 2 + lane // (LANES // 2)
    x_tap = [spread(ALONG_X, along[:, k] * scale) for k in range(2 * HALO + 1)]
    for at in range(3 * planes):
        weight = jnp.zeros((SUBS, LANES), jnp.float32)
        for k in range(-HALO, HALO + 1):
            if 0 <= at - planes + k < planes:
                weight = jnp.where(plane == at - planes + k, x_tap[k + HALO], weight)
        for b in range(BINS):
            w = np.float32((b + 0.5) / BINS)
            table[pl.ds((at * BINS + b) * SUBS, SUBS), :] = weight * jnp.where(upper, w, np.float32(1.0) - w)


def lookup_kernel(
    place, asked, field_hbm, out, field, table, prod, at_v, table_at_v, rows_of, at_s, table_at_s, sent, *, bands, planes, rows
):
    me = place[0]
    homes = asked.shape[0] // bands
    subs = lax.broadcasted_iota(jnp.int32, (SUBS, LANES), 0)
    fetch = pltpu.make_async_copy(field_hbm, field, sent.at[0])
    fetch.start()

    def read_row(row, _):
        cell, z, b = asked[row, 0:1, :], asked[row, 1:2, :], asked[row, 2:3, :]
        band = row // homes
        at = jnp.where(cell >= 0, (band - me + 1) * planes + cell // rows, 0)
        at_v[pl.ds(row, 1), :] = z * 4
        table_at_v[pl.ds(row, 1), :] = (at * BINS + b) * SUBS
        rows_of[pl.ds(row, 1), :] = cell % rows
        return 0

    lax.fori_loop(0, bands * homes, read_row, 0, unroll=4)
    moves = [pltpu.make_async_copy(at_v, at_s, sent.at[1]), pltpu.make_async_copy(table_at_v, table_at_s, sent.at[2])]
    for move in moves:
        move.start()
    fill_table(table, planes)
    for move in moves:
        move.wait()
    fetch.wait()

    def multiply(row, slot):
        for j in range(LANES):
            w_at = pl.multiple_of(table_at_s[row, j], SUBS)
            prod[slot, pl.ds(j * SUBS, SUBS), :] = field[pl.ds(at_s[row, j], SUBS), :] * table[pl.ds(w_at, SUBS), :]

    def reduce(row, slot):
        groups = []
        for i in range(LANES // SUBS):
            total = prod[slot, pl.ds(i * SUBS * SUBS, SUBS, stride=SUBS), :]
            for s in range(1, SUBS):
                total = total + prod[slot, pl.ds(i * SUBS * SUBS + s, SUBS, stride=SUBS), :]
            groups.append(total)
        flipped = jnp.concatenate(groups, axis=0).T
        mine = rows_of[pl.ds(row, 1), :] == subs
        for a in range(6):
            v = flipped[a * 8 : a * 8 + 8] + flipped[64 + a * 8 : 64 + a * 8 + 8]
            out[row, a, :] = jnp.sum(jnp.where(mine, v, 0.0), axis=0)

    first = jnp.maximum(me - 1, 0) * homes
    last = jnp.minimum(me + 2, bands) * homes

    def no_row(row, _):
        out[row] = jnp.zeros((6, LANES), jnp.float32)
        return 0

    lax.fori_loop(0, first, no_row, 0)

    multiply(first, 0)

    def two_rows(i, _):
        row = first + 2 * i
        multiply(row + 1, 1)
        reduce(row, 0)
        multiply(jnp.minimum(row + 2, last - 1), 0)
        reduce(row + 1, 1)
        return 0

    lax.fori_loop(0, (last - first) // 2, two_rows, 0)
    lax.fori_loop(last, bands * homes, no_row, 0)


def in_vmem(x):
    return pltpu.with_memory_space_constraint(x, pltpu.VMEM)


def body(potential, gal_cells, gal_z, gal_bins, gal_counts):
    bands = lax.axis_size("gx")
    homes = lax.axis_size("yz")
    planes, rows, depth = potential.shape
    tiles, slots = gal_cells.shape[2:]
    assert planes == SUBS and rows == SUBS and slots == LANES and homes % 2 == 0
    vmem = pl.BlockSpec(memory_space=pltpu.VMEM)
    smem = pl.BlockSpec(memory_space=pltpu.SMEM)

    by_row = potential.transpose(1, 0, 2)
    up = [(i, i + 1) for i in range(homes - 1)]
    down = [(j, i) for i, j in up]
    before = lax.ppermute(by_row[rows - HALO :], "yz", up)
    after = lax.ppermute(by_row[:HALO], "yz", down)

    slot_index = lax.broadcasted_iota(jnp.int32, (1, 1, tiles, slots), 3)
    gal_cells = jnp.where(slot_index < gal_counts[..., None], gal_cells, -1)
    asked = jnp.concatenate([gal_cells, gal_z, gal_bins], axis=0).reshape(3, tiles, slots).transpose(1, 0, 2)
    asked = jnp.broadcast_to(asked[None], (bands, tiles, 3, slots)).reshape(bands * tiles, 3, slots)
    asked = lax.all_to_all(asked, ("gx", "yz"), split_axis=0, concat_axis=0, tiled=True)

    chunks = 8
    field_shape = (depth * 4 + SUBS, LANES)
    mid_shape = (depth * 4 + 8 * SUBS, LANES)
    hbm = pl.BlockSpec(memory_space=pltpu.HBM)
    field = pl.pallas_call(
        functools.partial(field_kernel, rows=rows, depth=depth, chunks=chunks),
        out_shape=pltpu.HBM(field_shape, jnp.float32),
        in_specs=[vmem] * 3,
        out_specs=hbm,
        scratch_shapes=[
            pltpu.VMEM(mid_shape, jnp.float32),
            pltpu.VMEM(mid_shape, jnp.float32),
            pltpu.VMEM((2, 3 * rows * SUBS, LANES), jnp.float32),
            pltpu.VMEM(field_shape, jnp.float32),
            pltpu.SemaphoreType.DMA((chunks + 1,)),
        ],
        compiler_params=pltpu.CompilerParams(vmem_limit_bytes=24 << 20),
    )(in_vmem(before), in_vmem(by_row), in_vmem(after))

    me = lax.axis_index("gx")
    queries = (bands * homes, slots)
    served = pl.pallas_call(
        functools.partial(lookup_kernel, bands=bands, planes=planes, rows=rows),
        out_shape=jax.ShapeDtypeStruct((bands * homes, 6, slots), jnp.float32),
        in_specs=[smem, vmem, hbm],
        out_specs=vmem,
        scratch_shapes=[
            pltpu.VMEM(field_shape, jnp.float32),
            pltpu.VMEM((3 * planes * BINS * SUBS, LANES), jnp.float32),
            pltpu.VMEM((2, LANES * SUBS, LANES), jnp.float32),
            pltpu.VMEM(queries, jnp.int32),
            pltpu.VMEM(queries, jnp.int32),
            pltpu.VMEM(queries, jnp.int32),
            pltpu.SMEM(queries, jnp.int32),
            pltpu.SMEM(queries, jnp.int32),
            pltpu.SemaphoreType.DMA((3,)),
        ],
        compiler_params=pltpu.CompilerParams(vmem_limit_bytes=24 << 20),
    )(me.reshape(1), asked, pltpu.with_memory_space_constraint(field, pltpu.HBM))

    returned = lax.all_to_all(served, ("gx", "yz"), split_axis=0, concat_axis=0, tiled=True)
    total = jnp.sum(returned.reshape(bands, tiles, 6, slots), axis=0)
    return total.transpose(1, 0, 2).reshape(6, 1, 1, tiles * slots)


def solution(mesh):
    return jax.shard_map(
        body,
        mesh=mesh,
        in_specs=(
            P("gx", "yz", None),
            P("gx", "yz", None, None),
            P("gx", "yz", None, None),
            P("gx", "yz", None, None),
            P("gx", "yz", None),
        ),
        out_specs=P(None, "gx", "yz", None),
        check_vma=False,
    )
```

time: 60.2 us -> 45.6 us (0.76)
  blocking collectives: 0 us -> 13.9 us
  starting transfers between devices: 22.7 us -> 12.9 us
  waiting for transfers between devices: 10.7 us -> 1.18 us
  Pallas kernels: 20.8 us -> 13.1 us
  local copies, waits for them, and re-layouts: 3.99 us -> 2.67 us
    all_to_all x0 -> x1, blocking collectives: none -> 13.9 us  [body(): lax.all_to_all(served, ('gx', 'yz'), split_axis=0, concat_axis=0, tiled=T...]
    all_to_all x1 -> x0, starting transfers between devices: 11.9 us -> none  [body(): lax.all_to_all(served, ('gx', 'yz'), split_axis=0, concat_axis=0, tiled=T...]
    all_to_all x1 -> x0, waiting for transfers between devices: 8.08 us -> none  [body(): lax.all_to_all(served, ('gx', 'yz'), split_axis=0, concat_axis=0, tiled=T...]
    pallas_call x1, Pallas kernels: 11.5 us -> 6.18 us  [body(): pl.pallas_call(functools.partial(field_kernel, rows=rows, depth=depth, ch...]
    pallas_call x1, Pallas kernels: 9.27 us -> 6.91 us  [body(): pl.pallas_call(functools.partial(lookup_kernel, bands=bands, planes=plane...]
    all_to_all x1, starting transfers between devices: 7.33 us -> 9.17 us  [body(): lax.all_to_all(asked, ('gx', 'yz'), split_axis=0, concat_axis=0, tiled=True)]
    unnamed x9 -> x1, local copies, waits for them, and re-layouts: 2.61 us -> 1.35 us
    all_to_all x1, waiting for transfers between devices: 2.42 us -> 1.17 us  [body(): lax.all_to_all(asked, ('gx', 'yz'), split_axis=0, concat_axis=0, tiled=True)]
  transfers between devices with their start and end apart: 4 -> 3, of which waited for: 3 -> 1; matrix products, arithmetic and copies ran while one was open for 4% -> 5% of each run, Pallas kernels for 0% -> 14%
where the time goes in v2:
time: 45.6 us; the launch traced here: 45.3 us
  blocking collectives  13.9 us (30%)
  Pallas kernels  13.1 us (29%)
  starting transfers between devices  12.9 us (28%)
  local copies, waits for them, and re-layouts  2.67 us (6%)
  other arithmetic  1.48 us (3%)
  waiting for transfers between devices  1.18 us (3%)
    all_to_all x1, blocking collectives, body(): lax.all_to_all(served, ('gx', 'yz'), split_axis=0, concat_axis=0, tiled=T...  13.9 us
    all_to_all x1, starting transfers between devices, body(): lax.all_to_all(asked, ('gx', 'yz'), split_axis=0, concat_axis=0, tiled=True)  9.17 us
    pallas_call x1, Pallas kernels, body(): pl.pallas_call(functools.partial(lookup_kernel, bands=bands, planes=plane...  6.91 us
    pallas_call x1, Pallas kernels, body(): pl.pallas_call(functools.partial(field_kernel, rows=rows, depth=depth, ch...  6.18 us
    ppermute x1, starting transfers between devices, body(): before = lax.ppermute(by_row[rows - HALO:], 'yz', up)  2.42 us
    unnamed x1, local copies, waits for them, and re-layouts  1.35 us
    ppermute x1, starting transfers between devices, body(): after = lax.ppermute(by_row[:HALO], 'yz', down)  1.29 us
    all_to_all x1, waiting for transfers between devices, body(): lax.all_to_all(asked, ('gx', 'yz'), split_axis=0, concat_axis=0, tiled=True)  1.17 us
  transfers between devices with their start and end apart: 3, of which 1 were waited for; matrix products, arithmetic and copies ran while one was open for 5% of the time, Pallas kernels for 14%

profile of v2, /device:TPU:0, one launch (start us, length us, event | category | flops | bytes accessed | tf_op | source)
XLA Modules:
  0.0 45.3 jit_solution(5764804416883575738)
XLA Ops:
  0.0 1.3 %copy.14 = f32[8,8,2048]{2,0,1:T(8,128)S(1)} copy(f32[8,8,2048]{2,1,0:T(8,128)} %param.5) | data formatting | bytes 1048576 | tf_op args[0]
  1.4 0.1 fusion.1
  1.4 2.4 %collective-permute-start = (f32[6,8,2048]{2,1,0:T(8,128)S(1)}, f32[6,8,2048]{2,1,0:T(8,128)S(1)}, u32[]{:S(2)}, u32[]{:S(2)}) collective-permute-start(f32[6,8,2048]{2,1,0:T(8,128)S(1)} %get-tuple-element.6), channel_id=1, source_target_pairs={{0,1},{1,2},{2,3},{3,4},{4,5},{5,6},{6,7},{8,9},{9,10},{10,11},{11... | collective-permute-start | bytes 1179656 | tf_op jit(solution)/shard_map/ppermute | solution.py:231
  3.9 1.3 %collective-permute-start.1 = (f32[6,8,2048]{2,1,0:T(8,128)S(1)}, f32[6,8,2048]{2,1,0:T(8,128)S(1)}, u32[]{:S(2)}, u32[]{:S(2)}) collective-permute-start(f32[6,8,2048]{2,1,0:T(8,128)S(1)} %get-tuple-element.5), channel_id=1, source_target_pairs={{1,0},{2,1},{3,2},{4,3},{5,4},{6,5},{7,6},{9,8},{10,9},{11,10},{12... | collective-permute-start | bytes 1179656 | tf_op jit(solution)/shard_map/ppermute | solution.py:232
  5.2 0.8 %fusion = s32[1,1,8,128]{3,2,1,0:T(8,128)S(1)} fusion(s32[1,1,8,128]{3,2,1,0:T(8,128)} %param.6, s32[8]{0:T(128)} %bitcast.18), kind=kLoop, calls=%fused_computation.3 | loop fusion | flops 2048 | bytes 8224 | tf_op jit(solution)/shard_map/jit(_where)/select_n | solution.py:235
  5.9 0.7 %add_bitcast_fusion = s32[8,3,128]{2,0,1:T(8,128)S(1)} fusion(s32[1,1,8,128]{3,2,1,0:T(8,128)} %param.8, s32[1,1,8,128]{3,2,1,0:T(8,128)} %param.7, s32[1,1,8,128]{3,2,1,0:T(8,128)S(1)} %fusion), kind=kLoop, calls=%fused_computation.1 | loop fusion | flops 6144 | bytes 24576 | tf_op jit(solution)/shard_map/transpose | solution.py:236
  6.6 0.6 %broadcast_in_dim.12 = s32[4,8,3,128]{3,2,1,0:T(4,128)} broadcast(s32[8,3,128]{2,1,0:T(4,128)S(1)} %copy.10), dimensions={1,2,3} | broadcast | bytes 61440 | tf_op jit(solution)/shard_map/broadcast_in_dim | solution.py:237
  7.2 9.2 %all-to-all-start = ((s32[32,3,128]{2,1,0:T(4,128)}), s32[32,3,128]{2,1,0:T(4,128)S(1)}, u32[]{:S(2)}, u32[]{:S(2)}) async-start(s32[32,3,128]{2,1,0:T(4,128)} %bitcast.4), calls=%async_computation | async-start | bytes 131072 | tf_op jit(solution)/shard_map/all_to_all | solution.py:238
  16.4 0.0 collective-permute-done.before
  16.4 0.0 collective-permute-done.1.after
  16.5 6.2 %shard_map.58.field_hbm = f32[8200,128]{1,0:T(8,128)} custom-call(f32[6,8,2048]{2,1,0:T(8,128)S(1)} %collective-permute-done.before, f32[8,8,2048]{2,1,0:T(8,128)S(1)} %bitcast.15, f32[6,8,2048]{2,1,0:T(8,128)S(1)} %collective-permute-done.1.after), custom_call_target="tpu_custom_call" | custom-call | tf_op jit(solution)/shard_map/pallas_call | solution.py:244
  22.6 1.2 %all-to-all-done.asked = s32[32,3,128]{2,1,0:T(4,128)S(1)} async-done(((s32[32,3,128]{2,1,0:T(4,128)}), s32[32,3,128]{2,1,0:T(4,128)S(1)}, u32[]{:S(2)}, u32[]{:S(2)}) %all-to-all-start) | async-done | bytes 49184 | tf_op jit(solution)/shard_map/all_to_all | solution.py:238
  23.8 6.9 %shard_map.59 = f32[32,6,128]{2,1,0:T(8,128)S(1)} custom-call(s32[1]{0:T(128)} %bitcast.place, s32[32,3,128]{2,1,0:T(4,128)S(1)} %all-to-all-done.asked, f32[8200,128]{1,0:T(8,128)} %shard_map.58.field_hbm), custom_call_target="tpu_custom_call" | custom-call | tf_op jit(solution)/shard_map/pallas_call | solution.py:261
  30.7 13.9 %all_to_all.10 = f32[32,6,128]{2,1,0:T(8,128)S(1)} all-to-all(f32[32,6,128]{2,1,0:T(8,128)S(1)} %shard_map.59), channel_id=1, replica_groups=mesh['gx'=4,'yz'=8] {'gx','yz'}, dimensions={0} | all-to-all | bytes 196608 | tf_op jit(solution)/shard_map/all_to_all | solution.py:280
  44.6 0.6 %copy.12 = f32[6,1,1,1024]{3,2,1,0:T(1,128)} copy(f32[6,1,1,1024]{3,0,2,1:T(8,128)S(1)} %bitcast.17) | data formatting | bytes 49152 | tf_op jit(solution)/shard_map/reshape | solution.py:282
  (2 shorter events, 0.0 us)
Async XLA Ops:
  1.4 15.0 %collective-permute-start = (f32[6,8,2048]{2,1,0:T(8,128)S(1)}, f32[6,8,2048]{2,1,0:T(8,128)S(1)}, u32[]{:S(2)}, u32[]{:S(2)}) collective-permute-start(f32[6,8,2048]{2,1,0:T(8,128)S(1)} %get-tuple-element.6), channel_id=1, source_target_pairs={{0,1},{1,2},{2,3},{3,4},{4,5},{5,6},{6,7},{8,9},{9,10},{10,11},{11... | collective-permute-start | bytes 1179656 | tf_op jit(solution)/shard_map/ppermute | solution.py:231
  3.9 12.6 %collective-permute-start.1 = (f32[6,8,2048]{2,1,0:T(8,128)S(1)}, f32[6,8,2048]{2,1,0:T(8,128)S(1)}, u32[]{:S(2)}, u32[]{:S(2)}) collective-permute-start(f32[6,8,2048]{2,1,0:T(8,128)S(1)} %get-tuple-element.5), channel_id=1, source_target_pairs={{1,0},{2,1},{3,2},{4,3},{5,4},{6,5},{7,6},{9,8},{10,9},{11,10},{12... | collective-permute-start | bytes 1179656 | tf_op jit(solution)/shard_map/ppermute | solution.py:232
  7.2 16.6 %all-to-all-start = ((s32[32,3,128]{2,1,0:T(4,128)}), s32[32,3,128]{2,1,0:T(4,128)S(1)}, u32[]{:S(2)}, u32[]{:S(2)}) async-start(s32[32,3,128]{2,1,0:T(4,128)} %bitcast.4), calls=%async_computation | async-start | bytes 131072 | tf_op jit(solution)/shard_map/all_to_all | solution.py:238

commit v3 on v2

v3 whole, which is shorter than its diff:
```python
import functools

import jax
import jax.numpy as jnp
import numpy as np
from jax import lax
from jax.experimental import pallas as pl
from jax.experimental.pallas import tpu as pltpu
from jax.sharding import PartitionSpec as P


HALO = 6
BINS = 8
LANES = 128
SUBS = 8
CELL = 3
HELD = ((0, 3), (4, 5), (2, 1))
ALONG_X = (2, 0, 0, 1, 1, 0)


def taps():
    offsets = np.arange(-HALO, HALO + 1).astype(np.float32)
    sigma = np.float32(HALO / 3.0)
    smooth = np.exp(-offsets * offsets / (2 * sigma * sigma)).astype(np.float32)
    smooth = smooth / np.sum(smooth, dtype=np.float32)
    first = offsets / (sigma * sigma) * smooth
    second = (offsets * offsets / sigma**4 - 1 / (sigma * sigma)) * smooth
    return np.stack([smooth, first, second]).astype(np.float32)


def send_kernel(
    parity, counts_in, cells_in, zeds_in, bins_in, own_in, pair_out, next_out, asked_out, hold,
    counts, cells, zeds, bins, own, asked, came, gone, *, bands, rows
):
    fetches = [pltpu.make_async_copy(own_in.at[x], own.at[x], came.at[x]) for x in range(own.shape[0])]
    small = ((counts_in, counts), (cells_in, cells), (zeds_in, zeds), (bins_in, bins))
    small = [pltpu.make_async_copy(a, b, came.at[own.shape[0] + i]) for i, (a, b) in enumerate(small)]
    for copy in small + fetches:
        copy.start()
    for copy in small:
        copy.wait()
    tiles, slots = cells.shape
    slot = lax.broadcasted_iota(jnp.int32, (1, slots), 1)
    for t in range(tiles):
        cell = jnp.where(slot < counts[0, t], cells[t : t + 1, :], -1)
        query = jnp.concatenate([cell, zeds[t : t + 1, :], bins[t : t + 1, :]], axis=0)
        for band in range(bands):
            asked[band * tiles + t] = query
    moves = [pltpu.make_async_copy(asked, asked_out, gone.at[2, 0])]
    moves[0].start()
    for copy in fetches:
        copy.wait()
    to_pair = (rows - HALO) * (1 - parity[0])
    to_next = (rows - HALO) * parity[0]
    for y in range(HALO):
        moves.append(pltpu.make_async_copy(own.at[:, to_pair + y, :], pair_out.at[y], gone.at[0, y]))
        moves.append(pltpu.make_async_copy(own.at[:, to_next + y, :], next_out.at[y], gone.at[1, y]))
    for copy in moves[1:]:
        copy.start()
    for copy in moves:
        copy.wait()


def field_kernel(parity, pair_in, own_in, next_in, hold, field, before, after, own, mid_01, mid_02, came, *, rows, depth, chunks):
    along = taps()
    size = depth // chunks
    per = size // LANES
    planes = own_in.shape[0]

    def fetches(c, pair_to, next_to):
        zs = pl.ds(c * size, size)
        return [
            pltpu.make_async_copy(pair_in.at[:, :, zs], pair_to.at[:, :, zs], came.at[c, 0]),
            pltpu.make_async_copy(next_in.at[:, :, zs], next_to.at[:, :, zs], came.at[c, 1]),
        ] + [pltpu.make_async_copy(own_in.at[x, :, zs], own.at[:, x, zs], came.at[c, 2 + x]) for x in range(planes)]

    even = parity[0] == 0
    for c in range(chunks):
        for copy in fetches(c, after, before)[2:]:
            copy.start()

        @pl.when(even)
        def _():
            for copy in fetches(c, after, before)[:2]:
                copy.start()

        @pl.when(jnp.logical_not(even))
        def _():
            for copy in fetches(c, before, after)[:2]:
                copy.start()

    def along_y(block, _):
        z0 = pl.multiple_of(block * LANES, LANES)
        zs = pl.ds(z0, LANES)
        u = [before[y, :, zs] for y in range(HALO)]
        u += [own[y, :, zs] for y in range(rows)]
        u += [after[y, :, zs] for y in range(HALO)]
        filtered = [[], [], []]
        for r in range(rows):
            c = u[r + HALO]
            smooth = c * along[0][HALO]
            second = c * along[2][HALO]
            first = None
            for k in range(1, HALO + 1):
                up, down = u[r + HALO + k], u[r + HALO - k]
                both = up + down
                smooth = smooth + both * along[0][HALO + k]
                second = second + both * along[2][HALO + k]
                part = (up - down) * along[1][HALO + k]
                first = part if first is None else first + part
            for f, v in enumerate((smooth, first, second)):
                filtered[f].append(v)
        mid_01[pl.ds(z0 + SUBS, LANES), :] = jnp.concatenate(filtered[0] + filtered[1], axis=0).T
        mid_02[pl.ds(z0 + SUBS, LANES), :] = jnp.concatenate(filtered[0] + filtered[2], axis=0).T
        return 0

    for c in range(chunks):
        for copy in fetches(c, after, before):
            copy.wait()
        lax.fori_loop(c * per, (c + 1) * per, along_y, 0, unroll=2)
    for buf in (mid_01, mid_02):
        buf[pl.ds(0, SUBS), :] = buf[pl.ds(depth, SUBS), :]
        buf[pl.ds(depth + SUBS, SUBS), :] = buf[pl.ds(SUBS, SUBS), :]

    n = 8
    lower = lax.broadcasted_iota(jnp.int32, (SUBS, LANES), 1) < LANES // 2
    mixed = [jnp.where(lower, along[2][HALO + k], along[0][HALO + k]) for k in range(HALO + 1)]

    def along_z(block, _):
        base = pl.multiple_of(block * (n * SUBS), n * SUBS)
        for j in range(n):
            at = base + SUBS * j + SUBS
            smooth = mid_01[pl.ds(at, SUBS), :] * along[0][HALO]
            first = None
            both = mid_02[pl.ds(at, SUBS), :] * mixed[0]
            for k in range(1, HALO + 1):
                up, down = mid_01[pl.ds(at + k, SUBS), :], mid_01[pl.ds(at - k, SUBS), :]
                smooth = smooth + (up + down) * along[0][HALO + k]
                part = (up - down) * along[1][HALO + k]
                first = part if first is None else first + part
                up, down = mid_02[pl.ds(at + k, SUBS), :], mid_02[pl.ds(at - k, SUBS), :]
                both = both + (up + down) * mixed[k]
            for i, v in enumerate((smooth, first, both)):
                field[pl.ds((base + SUBS * j) * CELL + i, SUBS, stride=CELL), :] = v
        return 0

    lax.fori_loop(0, depth // (n * SUBS), along_z, 0)
    field[pl.ds(depth * CELL, SUBS), :] = field[pl.ds(0, SUBS), :]


def fill_table(table, planes):
    along = taps()
    scale = np.float32((HALO / 3.0) ** 2)
    sub = lax.broadcasted_iota(jnp.int32, (SUBS, LANES), 0)
    lane = lax.broadcasted_iota(jnp.int32, (SUBS, LANES), 1)
    plane = lane % planes
    half = lane // (LANES // 2)

    def x_tap(k):
        out = jnp.zeros((SUBS, LANES), jnp.float32)
        for i, pair in enumerate(HELD):
            for h, a in enumerate(pair):
                held = ((sub == i) | (sub == i + CELL)) & (half == h)
                out = jnp.where(held, along[ALONG_X[a]][k + HALO] * scale, out)
        return out

    x_taps = [x_tap(k) for k in range(-HALO, HALO + 1)]
    for at in range(3 * planes):
        weight = jnp.zeros((SUBS, LANES), jnp.float32)
        for k in range(-HALO, HALO + 1):
            if 0 <= at - planes + k < planes:
                weight = jnp.where(plane == at - planes + k, x_taps[k + HALO], weight)
        for b in range(BINS):
            w = np.float32((b + 0.5) / BINS)
            table[pl.ds((at * BINS + b) * SUBS, SUBS), :] = weight * jnp.where(sub >= CELL, w, np.float32(1.0) - w)


def woven(many, few):
    each = max(len(many) // max(len(few), 1), 1)
    few = list(few)
    for i, step in enumerate(many):
        if i % each == 0 and few:
            few.pop(0)()
        step()
    for step in few:
        step()


def lookup_kernel(
    place, asked, field, out, table, prod, sums, at_v, table_at_v, rows_of, at_s, table_at_s, sent, *, bands, planes, rows
):
    me = place[0]
    homes = asked.shape[0] // bands

    def read_row(row, _):
        cell, z, b = asked[row, 0:1, :], asked[row, 1:2, :], asked[row, 2:3, :]
        band = row // homes
        at = jnp.where(cell >= 0, (band - me + 1) * planes + cell // rows, 0)
        at_v[pl.ds(row, 1), :] = z * CELL
        table_at_v[pl.ds(row, 1), :] = (at * BINS + b) * SUBS
        rows_of[pl.ds(row, 1), :] = cell % rows
        return 0

    lax.fori_loop(0, bands * homes, read_row, 0, unroll=4)
    moves = [pltpu.make_async_copy(at_v, at_s, sent.at[0]), pltpu.make_async_copy(table_at_v, table_at_s, sent.at[1])]
    for move in moves:
        move.start()
    fill_table(table, planes)
    for move in moves:
        move.wait()

    def multiply(row, slot):
        def one_group(i):
            for j in range(i * SUBS, (i + 1) * SUBS):
                w_at = pl.multiple_of(table_at_s[row, j], SUBS)
                prod[slot, pl.ds(j * SUBS, SUBS), :] = field[pl.ds(at_s[row, j], SUBS), :] * table[pl.ds(w_at, SUBS), :]

        return [functools.partial(one_group, i) for i in range(LANES // SUBS)]

    def reduce(slot):
        def one_group(i):
            for c in range(CELL):
                here = prod[slot, pl.ds(i * SUBS * SUBS + c, SUBS, stride=SUBS), :]
                beyond = prod[slot, pl.ds(i * SUBS * SUBS + CELL + c, SUBS, stride=SUBS), :]
                sums[slot, c, pl.ds(i * SUBS, SUBS), :] = here + beyond

        return [functools.partial(one_group, i) for i in range(LANES // SUBS)]

    def finish(row, slot):
        mine = jnp.broadcast_to(rows_of[pl.ds(row, 1), :], (SUBS, LANES))
        for c, pair in enumerate(HELD):
            flipped = sums[slot, c].T
            for h, a in enumerate(pair):
                at = h * rows * SUBS
                picked = flipped[at : at + SUBS]
                for r in range(1, rows):
                    picked = jnp.where(mine == r, flipped[at + r * SUBS : at + (r + 1) * SUBS], picked)
                out[row, a, :] = jnp.sum(picked, axis=0)

    first = jnp.maximum(me - 1, 0) * homes
    last = jnp.minimum(me + 2, bands) * homes

    def no_row(row, _):
        out[row] = jnp.zeros((6, LANES), jnp.float32)
        return 0

    lax.fori_loop(0, first, no_row, 0)

    sums[1] = jnp.zeros((CELL, LANES, LANES), jnp.float32)
    woven(multiply(first, 0), [])

    def two_rows(i, _):
        row = first + 2 * i
        finish(jnp.maximum(row - 1, first), 1)
        woven(multiply(row + 1, 1), reduce(0))
        finish(row, 0)
        woven(multiply(jnp.minimum(row + 2, last - 1), 0), reduce(1))
        return 0

    lax.fori_loop(0, (last - first) // 2, two_rows, 0)
    finish(last - 1, 1)
    lax.fori_loop(last, bands * homes, no_row, 0)


def in_hbm(x):
    return pltpu.with_memory_space_constraint(x, pltpu.HBM)


def in_vmem(x):
    return pltpu.with_memory_space_constraint(x, pltpu.VMEM)


def body(potential, gal_cells, gal_z, gal_bins, gal_counts):
    bands = lax.axis_size("gx")
    homes = lax.axis_size("yz")
    planes, rows, depth = potential.shape
    tiles, slots = gal_cells.shape[2:]
    assert planes == SUBS and rows == SUBS and slots == LANES and homes % 2 == 0
    vmem = pl.BlockSpec(memory_space=pltpu.VMEM)
    smem = pl.BlockSpec(memory_space=pltpu.SMEM)

    parity = (lax.axis_index("yz") % 2).reshape(1)
    hbm = pl.BlockSpec(memory_space=pltpu.HBM)
    field_shape = (depth * CELL + SUBS, LANES)
    halo_shape = (HALO, planes, depth)
    pair_out, next_out, asked, hold = pl.pallas_call(
        functools.partial(send_kernel, bands=bands, rows=rows),
        out_shape=(
            jax.ShapeDtypeStruct(halo_shape, jnp.float32),
            jax.ShapeDtypeStruct(halo_shape, jnp.float32),
            jax.ShapeDtypeStruct((bands * tiles, 3, slots), jnp.int32),
            pltpu.VMEM(field_shape, jnp.float32),
        ),
        in_specs=[smem] + [hbm] * 5,
        out_specs=(hbm, hbm, hbm, vmem),
        scratch_shapes=[
            pltpu.SMEM((1, tiles), jnp.int32),
            pltpu.VMEM((tiles, slots), jnp.int32),
            pltpu.VMEM((tiles, slots), jnp.int32),
            pltpu.VMEM((tiles, slots), jnp.int32),
            pltpu.VMEM(potential.shape, jnp.float32),
            pltpu.VMEM((bands * tiles, 3, slots), jnp.int32),
            pltpu.SemaphoreType.DMA((planes + 4,)),
            pltpu.SemaphoreType.DMA((3, HALO)),
        ],
        compiler_params=pltpu.CompilerParams(vmem_limit_bytes=8 << 20),
    )(
        parity,
        in_hbm(gal_counts.reshape(1, tiles)),
        in_hbm(gal_cells.reshape(tiles, slots)),
        in_hbm(gal_z.reshape(tiles, slots)),
        in_hbm(gal_bins.reshape(tiles, slots)),
        in_hbm(potential),
    )

    swap = lambda first: [p for i in range(first, homes - 1, 2) for p in ((i, i + 1), (i + 1, i))]
    pair_in = lax.ppermute(pair_out, "yz", swap(0))
    next_in = lax.ppermute(next_out, "yz", swap(1))
    asked = lax.all_to_all(asked, ("gx", "yz"), split_axis=0, concat_axis=0, tiled=True)

    chunks = 4
    mid_shape = (depth + 2 * SUBS, LANES)
    field = pl.pallas_call(
        functools.partial(field_kernel, rows=rows, depth=depth, chunks=chunks),
        out_shape=pltpu.VMEM(field_shape, jnp.float32),
        in_specs=[smem, hbm, hbm, hbm, vmem],
        out_specs=vmem,
        input_output_aliases={4: 0},
        scratch_shapes=[
            pltpu.VMEM(halo_shape, jnp.float32),
            pltpu.VMEM(halo_shape, jnp.float32),
            pltpu.VMEM((rows, planes, depth), jnp.float32),
            pltpu.VMEM(mid_shape, jnp.float32),
            pltpu.VMEM(mid_shape, jnp.float32),
            pltpu.SemaphoreType.DMA((chunks, 2 + planes)),
        ],
        compiler_params=pltpu.CompilerParams(vmem_limit_bytes=24 << 20),
    )(parity, in_hbm(pair_in), in_hbm(potential), in_hbm(next_in), in_vmem(hold))

    me = lax.axis_index("gx")
    queries = (bands * homes, slots)
    served = pl.pallas_call(
        functools.partial(lookup_kernel, bands=bands, planes=planes, rows=rows),
        out_shape=jax.ShapeDtypeStruct((bands * homes, 6, slots), jnp.float32),
        in_specs=[smem, vmem, vmem],
        out_specs=vmem,
        scratch_shapes=[
            pltpu.VMEM((3 * planes * BINS * SUBS, LANES), jnp.float32),
            pltpu.VMEM((2, LANES * SUBS + SUBS, LANES), jnp.float32),
            pltpu.VMEM((2, CELL, LANES, LANES), jnp.float32),
            pltpu.VMEM(queries, jnp.int32),
            pltpu.VMEM(queries, jnp.int32),
            pltpu.VMEM(queries, jnp.int32),
            pltpu.SMEM(queries, jnp.int32),
            pltpu.SMEM(queries, jnp.int32),
            pltpu.SemaphoreType.DMA((2,)),
        ],
        compiler_params=pltpu.CompilerParams(vmem_limit_bytes=24 << 20),
    )(me.reshape(1), asked, in_vmem(field))

    returned = lax.all_to_all(served, ("gx", "yz"), split_axis=0, concat_axis=0, tiled=True)
    total = jnp.sum(returned.reshape(bands, tiles, 6, slots), axis=0)
    return total.transpose(1, 0, 2).reshape(6, 1, 1, tiles * slots)


def solution(mesh):
    return jax.shard_map(
        body,
        mesh=mesh,
        in_specs=(
            P("gx", "yz", None),
            P("gx", "yz", None, None),
            P("gx", "yz", None, None),
            P("gx", "yz", None, None),
            P("gx", "yz", None),
        ),
        out_specs=P(None, "gx", "yz", None),
        check_vma=False,
    )
```

time: 45.6 us -> 39.3 us (0.86)
  starting transfers between devices: 12.9 us -> 9.87 us
  local copies, waits for them, and re-layouts: 2.67 us -> 0.63 us
  other arithmetic: 1.48 us -> 0.01 us
  waiting for transfers between devices: 1.18 us -> 2.14 us
    pallas_call x0 -> x1, Pallas kernels: none -> 2.27 us  [body(): pl.pallas_call(functools.partial(send_kernel, bands=bands, rows=rows), ou...]
    ppermute x2, starting transfers between devices: 3.71 us -> 1.98 us  [the longest x1 1.42 us: body(): next_in = lax.ppermute(next_out, 'yz', swap(1))]
    pallas_call x1, Pallas kernels: 6.91 us -> 5.29 us  [body(): pl.pallas_call(functools.partial(lookup_kernel, bands=bands, planes=plane...]
    unnamed x1 -> x0, local copies, waits for them, and re-layouts: 1.35 us -> none
    all_to_all x1, starting transfers between devices: 9.17 us -> 7.89 us  [body(): lax.all_to_all(asked, ('gx', 'yz'), split_axis=0, concat_axis=0, tiled=True)]
    pallas_call x1, Pallas kernels: 6.18 us -> 5.22 us  [body(): pl.pallas_call(functools.partial(field_kernel, rows=rows, depth=depth, ch...]
    all_to_all x1, waiting for transfers between devices: 1.17 us -> 2.13 us  [body(): lax.all_to_all(asked, ('gx', 'yz'), split_axis=0, concat_axis=0, tiled=True)]
    select_n x1 -> x0, other arithmetic: 0.76 us -> none  [body(): gal_cells = jnp.where(slot_index < gal_counts[..., None], gal_cells, -1)]
  transfers between devices with their start and end apart: 3 -> 3, of which waited for: 1 -> 1; matrix products, arithmetic and copies ran while one was open for 5% -> 0% of each run, Pallas kernels for 14% -> 13%
where the time goes in v3:
time: 39.3 us; the launch traced here: 39.1 us
  blocking collectives  13.6 us (35%)
  Pallas kernels  12.8 us (33%)
  starting transfers between devices  9.87 us (25%)
  waiting for transfers between devices  2.14 us (5%)
  local copies, waits for them, and re-layouts  0.63 us (2%)
    all_to_all x1, blocking collectives, body(): lax.all_to_all(served, ('gx', 'yz'), split_axis=0, concat_axis=0, tiled=T...  13.6 us
    all_to_all x1, starting transfers between devices, body(): lax.all_to_all(asked, ('gx', 'yz'), split_axis=0, concat_axis=0, tiled=True)  7.89 us
    pallas_call x1, Pallas kernels, body(): pl.pallas_call(functools.partial(lookup_kernel, bands=bands, planes=plane...  5.29 us
    pallas_call x1, Pallas kernels, body(): pl.pallas_call(functools.partial(field_kernel, rows=rows, depth=depth, ch...  5.22 us
    pallas_call x1, Pallas kernels, body(): pl.pallas_call(functools.partial(send_kernel, bands=bands, rows=rows), ou...  2.27 us
    all_to_all x1, waiting for transfers between devices, body(): lax.all_to_all(asked, ('gx', 'yz'), split_axis=0, concat_axis=0, tiled=True)  2.13 us
    ppermute x1, starting transfers between devices, body(): next_in = lax.ppermute(next_out, 'yz', swap(1))  1.42 us
  transfers between devices with their start and end apart: 3, of which 1 were waited for; matrix products, arithmetic and copies ran while one was open for 0% of the time, Pallas kernels for 13%

profile of v3, /device:TPU:0, one launch (start us, length us, event | category | flops | bytes accessed | tf_op | source)
XLA Modules:
  0.0 39.1 jit_solution(16660034353718196992)
XLA Ops:
  0.0 2.3 %shard_map.55 = (f32[6,8,2048]{2,1,0:T(8,128)}, f32[6,8,2048]{2,1,0:T(8,128)}, s32[32,3,128]{2,1,0:T(4,128)}, f32[6152,128]{1,0:T(8,128)S(1)}) custom-call(s32[1]{0:T(128)} %bitcast.1.parity, s32[1,8]{1,0:T(1,128)} %bitcast.15, s32[8,128]{1,0:T(8,128)} %bitcast.12, s32[8,128]{1,0:T(8,128)} %bitcast.13, s32[8,128]{1,0:T(8,128)} %bitcast.14, f32[8,8,2048]{2,1,0:T(8,128)} %own_in.3), custom_call_target="tpu_custom_call" | custom-call | tf_op jit(solution)/shard_map/pallas_call | solution.py:286
  2.3 0.6 %collective-permute-start = (f32[6,8,2048]{2,1,0:T(8,128)}, f32[6,8,2048]{2,1,0:T(8,128)}, u32[]{:S(2)}, u32[]{:S(2)}) collective-permute-start(f32[6,8,2048]{2,1,0:T(8,128)} %get-tuple-element.10), channel_id=1, source_target_pairs={{0,1},{1,0},{2,3},{3,2},{4,5},{5,4},{6,7},{7,6},{8,9},{9,8},{10,11... | collective-permute-start | bytes 1179656 | tf_op jit(solution)/shard_map/ppermute | solution.py:317
  2.8 1.4 %collective-permute-start.1 = (f32[6,8,2048]{2,1,0:T(8,128)}, f32[6,8,2048]{2,1,0:T(8,128)}, u32[]{:S(2)}, u32[]{:S(2)}) collective-permute-start(f32[6,8,2048]{2,1,0:T(8,128)} %get-tuple-element.11), channel_id=1, source_target_pairs={{1,2},{2,1},{3,4},{4,3},{5,6},{6,5},{9,10},{10,9},{11,12},{12,11},... | collective-permute-start | bytes 1179656 | tf_op jit(solution)/shard_map/ppermute | solution.py:318
  4.3 7.9 %all-to-all-start = ((s32[32,3,128]{2,1,0:T(4,128)}), s32[32,3,128]{2,1,0:T(4,128)S(1)}, u32[]{:S(2)}, u32[]{:S(2)}) async-start(s32[32,3,128]{2,1,0:T(4,128)} %get-tuple-element.9), calls=%async_computation | async-start | bytes 131072 | tf_op jit(solution)/shard_map/all_to_all | solution.py:319
  12.2 0.0 collective-permute-done.pair_in
  12.2 0.0 collective-permute-done.1.next_in
  12.2 5.2 %shard_map.56.field = f32[6152,128]{1,0:T(8,128)S(1)} custom-call(s32[1]{0:T(128)} %bitcast.1.parity, f32[6,8,2048]{2,1,0:T(8,128)} %collective-permute-done.pair_in, f32[8,8,2048]{2,1,0:T(8,128)} %own_in.3, f32[6,8,2048]{2,1,0:T(8,128)} %collective-permute-done.1.next_in, f32[6152,128]{1,0:T(8,128)S(1)} %get-tuple-element.12.hold), custom_call_target="tpu_custom_call", output_to_operand_aliasing={{}: (4, {})} | custom-call | tf_op jit(solution)/shard_map/pallas_call | solution.py:323
  17.4 2.1 %all-to-all-done.asked = s32[32,3,128]{2,1,0:T(4,128)S(1)} async-done(((s32[32,3,128]{2,1,0:T(4,128)}), s32[32,3,128]{2,1,0:T(4,128)S(1)}, u32[]{:S(2)}, u32[]{:S(2)}) %all-to-all-start) | async-done | bytes 49184 | tf_op jit(solution)/shard_map/all_to_all | solution.py:319
  19.5 5.3 %shard_map.57 = f32[32,6,128]{2,1,0:T(8,128)S(1)} custom-call(s32[1]{0:T(128)} %bitcast.place, s32[32,3,128]{2,1,0:T(4,128)S(1)} %all-to-all-done.asked, f32[6152,128]{1,0:T(8,128)S(1)} %shard_map.56.field), custom_call_target="tpu_custom_call" | custom-call | tf_op jit(solution)/shard_map/pallas_call | solution.py:342
  24.8 13.6 %all_to_all.10 = f32[32,6,128]{2,1,0:T(8,128)S(1)} all-to-all(f32[32,6,128]{2,1,0:T(8,128)S(1)} %shard_map.57), channel_id=1, replica_groups=mesh['gx'=4,'yz'=8] {'gx','yz'}, dimensions={0} | all-to-all | bytes 196608 | tf_op jit(solution)/shard_map/all_to_all | solution.py:361
  38.4 0.6 %copy.7 = f32[6,1,1,1024]{3,2,1,0:T(1,128)} copy(f32[6,1,1,1024]{3,0,2,1:T(8,128)S(1)} %bitcast.11) | data formatting | bytes 49152 | tf_op jit(solution)/shard_map/reshape | solution.py:363
  (1 shorter events, 0.0 us)
Async XLA Ops:
  2.3 9.9 %collective-permute-start = (f32[6,8,2048]{2,1,0:T(8,128)}, f32[6,8,2048]{2,1,0:T(8,128)}, u32[]{:S(2)}, u32[]{:S(2)}) collective-permute-start(f32[6,8,2048]{2,1,0:T(8,128)} %get-tuple-element.10), channel_id=1, source_target_pairs={{0,1},{1,0},{2,3},{3,2},{4,5},{5,4},{6,7},{7,6},{8,9},{9,8},{10,11... | collective-permute-start | bytes 1179656 | tf_op jit(solution)/shard_map/ppermute | solution.py:317
  2.8 9.3 %collective-permute-start.1 = (f32[6,8,2048]{2,1,0:T(8,128)}, f32[6,8,2048]{2,1,0:T(8,128)}, u32[]{:S(2)}, u32[]{:S(2)}) collective-permute-start(f32[6,8,2048]{2,1,0:T(8,128)} %get-tuple-element.11), channel_id=1, source_target_pairs={{1,2},{2,1},{3,4},{4,3},{5,6},{6,5},{9,10},{10,9},{11,12},{12,11},... | collective-permute-start | bytes 1179656 | tf_op jit(solution)/shard_map/ppermute | solution.py:318
  4.3 15.3 %all-to-all-start = ((s32[32,3,128]{2,1,0:T(4,128)}), s32[32,3,128]{2,1,0:T(4,128)S(1)}, u32[]{:S(2)}, u32[]{:S(2)}) async-start(s32[32,3,128]{2,1,0:T(4,128)} %get-tuple-element.9), calls=%async_computation | async-start | bytes 131072 | tf_op jit(solution)/shard_map/all_to_all | solution.py:319

commit v4 on v3

--- a/solution.py
+++ b/solution.py
@@ -13,6 +13,7 @@
 BINS = 8
 LANES = 128
 SUBS = 8
+UNROLL = 4
 CELL = 3
 HELD = ((0, 3), (4, 5), (2, 1))
 ALONG_X = (2, 0, 0, 1, 1, 0)
@@ -148,33 +149,6 @@
     field[pl.ds(depth * CELL, SUBS), :] = field[pl.ds(0, SUBS), :]
 
 
-def fill_table(table, planes):
-    along = taps()
-    scale = np.float32((HALO / 3.0) ** 2)
-    sub = lax.broadcasted_iota(jnp.int32, (SUBS, LANES), 0)
-    lane = lax.broadcasted_iota(jnp.int32, (SUBS, LANES), 1)
-    plane = lane % planes
-    half = lane // (LANES // 2)
-
-    def x_tap(k):
-        out = jnp.zeros((SUBS, LANES), jnp.float32)
-        for i, pair in enumerate(HELD):
-            for h, a in enumerate(pair):
-                held = ((sub == i) | (sub == i + CELL)) & (half == h)
-                out = jnp.where(held, along[ALONG_X[a]][k + HALO] * scale, out)
-        return out
-
-    x_taps = [x_tap(k) for k in range(-HALO, HALO + 1)]
-    for at in range(3 * planes):
-        weight = jnp.zeros((SUBS, LANES), jnp.float32)
-        for k in range(-HALO, HALO + 1):
-            if 0 <= at - planes + k < planes:
-                weight = jnp.where(plane == at - planes + k, x_taps[k + HALO], weight)
-        for b in range(BINS):
-            w = np.float32((b + 0.5) / BINS)
-            table[pl.ds((at * BINS + b) * SUBS, SUBS), :] = weight * jnp.where(sub >= CELL, w, np.float32(1.0) - w)
-
-
 def woven(many, few):
     each = max(len(many) // max(len(few), 1), 1)
     few = list(few)
@@ -186,80 +160,81 @@
         step()
 
 
-def lookup_kernel(
-    place, asked, field, out, table, prod, sums, at_v, table_at_v, rows_of, at_s, table_at_s, sent, *, bands, planes, rows
-):
+def lookup_kernel(place, asked, field, out, found, at_v, plane_of, row_of, bin_of, at_s, sent, *, bands, planes, rows):
     me = place[0]
     homes = asked.shape[0] // bands
-
-    def read_row(row, _):
-        cell, z, b = asked[row, 0:1, :], asked[row, 1:2, :], asked[row, 2:3, :]
-        band = row // homes
-        at = jnp.where(cell >= 0, (band - me + 1) * planes + cell // rows, 0)
-        at_v[pl.ds(row, 1), :] = z * CELL
-        table_at_v[pl.ds(row, 1), :] = (at * BINS + b) * SUBS
-        rows_of[pl.ds(row, 1), :] = cell % rows
-        return 0
-
-    lax.fori_loop(0, bands * homes, read_row, 0, unroll=4)
-    moves = [pltpu.make_async_copy(at_v, at_s, sent.at[0]), pltpu.make_async_copy(table_at_v, table_at_s, sent.at[1])]
-    for move in moves:
-        move.start()
-    fill_table(table, planes)
-    for move in moves:
-        move.wait()
-
-    def multiply(row, slot):
+    first = jnp.maximum(me - 1, 0) * homes
+    last = jnp.minimum(me + 2, bands) * homes
+    along = taps()
+    scale = np.float32((HALO / 3.0) ** 2)
+    subs = lax.broadcasted_iota(jnp.int32, (SUBS, LANES), 0)
+
+    def read_rows(i, _):
+        for u in range(UNROLL):
+            row = first + UNROLL * i + u
+            cell, z, b = asked[row, 0:1, :], asked[row, 1:2, :], asked[row, 2:3, :]
+            at_v[pl.ds(row, 1), :] = z * CELL
+            plane_of[pl.ds(row, 1), :] = jnp.where(cell >= 0, (row // homes - me) * planes + cell // rows, -planes)
+            row_of[pl.ds(row, 1), :] = cell % rows
+            bin_of[pl.ds(row, 1), :] = b
+        return 0
+
+    lax.fori_loop(0, (last - first) // UNROLL, read_rows, 0)
+    move = pltpu.make_async_copy(at_v, at_s, sent)
+    move.start()
+
+    def no_row(row, _):
+        out[row] = jnp.zeros((6, LANES), jnp.float32)
+        return 0
+
+    lax.fori_loop(0, first, no_row, 0)
+    lax.fori_loop(last, bands * homes, no_row, 0)
+    move.wait()
+
+    def gather(row, slot):
         def one_group(i):
             for j in range(i * SUBS, (i + 1) * SUBS):
-                w_at = pl.multiple_of(table_at_s[row, j], SUBS)
-                prod[slot, pl.ds(j * SUBS, SUBS), :] = field[pl.ds(at_s[row, j], SUBS), :] * table[pl.ds(w_at, SUBS), :]
+                found[slot, pl.ds(j * SUBS, SUBS), :] = field[pl.ds(at_s[row, j], SUBS), :]
 
         return [functools.partial(one_group, i) for i in range(LANES // SUBS)]
 
-    def reduce(slot):
-        def one_group(i):
-            for c in range(CELL):
-                here = prod[slot, pl.ds(i * SUBS * SUBS + c, SUBS, stride=SUBS), :]
-                beyond = prod[slot, pl.ds(i * SUBS * SUBS + CELL + c, SUBS, stride=SUBS), :]
-                sums[slot, c, pl.ds(i * SUBS, SUBS), :] = here + beyond
-
-        return [functools.partial(one_group, i) for i in range(LANES // SUBS)]
-
     def finish(row, slot):
-        mine = jnp.broadcast_to(rows_of[pl.ds(row, 1), :], (SUBS, LANES))
-        for c, pair in enumerate(HELD):
-            flipped = sums[slot, c].T
-            for h, a in enumerate(pair):
-                at = h * rows * SUBS
-                picked = flipped[at : at + SUBS]
+        picked = {}
+
+        def turn(beyond, c):
+            at = beyond * CELL + c
+            groups = [found[slot, pl.ds(i * SUBS * SUBS + at, SUBS, stride=SUBS), :] for i in range(LANES // SUBS)]
+            flipped = jnp.concatenate(groups, axis=0).T
+            mine = jnp.broadcast_to(row_of[pl.ds(row, 1), :], (SUBS, LANES))
+            for h, a in enumerate(HELD[c]):
+                tiles = [flipped[(h * rows + r) * SUBS : (h * rows + r + 1) * SUBS] for r in range(rows)]
+                pick = tiles[0]
                 for r in range(1, rows):
-                    picked = jnp.where(mine == r, flipped[at + r * SUBS : at + (r + 1) * SUBS], picked)
-                out[row, a, :] = jnp.sum(picked, axis=0)
-
-    first = jnp.maximum(me - 1, 0) * homes
-    last = jnp.minimum(me + 2, bands) * homes
-
-    def no_row(row, _):
-        out[row] = jnp.zeros((6, LANES), jnp.float32)
-        return 0
-
-    lax.fori_loop(0, first, no_row, 0)
-
-    sums[1] = jnp.zeros((CELL, LANES, LANES), jnp.float32)
-    woven(multiply(first, 0), [])
-
-    def two_rows(i, _):
-        row = first + 2 * i
-        finish(jnp.maximum(row - 1, first), 1)
-        woven(multiply(row + 1, 1), reduce(0))
-        finish(row, 0)
-        woven(multiply(jnp.minimum(row + 2, last - 1), 0), reduce(1))
-        return 0
-
-    lax.fori_loop(0, (last - first) // 2, two_rows, 0)
-    finish(last - 1, 1)
-    lax.fori_loop(last, bands * homes, no_row, 0)
+                    pick = jnp.where(mine == r, tiles[r], pick)
+                picked[beyond, a] = pick
+
+        def total():
+            away = subs - plane_of[pl.ds(row, 1), :]
+            weights = [jnp.zeros((SUBS, LANES), jnp.float32)] * 3
+            for k in range(-HALO, HALO + 1):
+                here = away == k
+                weights = [jnp.where(here, along[f][k + HALO] * scale, w) for f, w in enumerate(weights)]
+            w = (bin_of[pl.ds(row, 1), :].astype(jnp.float32) + 0.5) * (1.0 / BINS)
+            for a in range(6):
+                value = (1.0 - w) * picked[0, a] + w * picked[1, a]
+                out[row, a, :] = jnp.sum(value * weights[ALONG_X[a]], axis=0)
+
+        return [functools.partial(turn, beyond, c) for c in range(CELL) for beyond in range(2)] + [total]
+
+    woven(gather(first, 0), [])
+
+    def some_rows(i, _):
+        for u in range(UNROLL):
+            row = first + UNROLL * i + u
+            woven(gather(jnp.minimum(row + 1, last - 1), (u + 1) % 2), finish(row, u % 2))
+        return 0
+
+    lax.fori_loop(0, (last - first) // UNROLL, some_rows, 0)
 
 
 def in_hbm(x):
@@ -275,7 +250,7 @@
     homes = lax.axis_size("yz")
     planes, rows, depth = potential.shape
     tiles, slots = gal_cells.shape[2:]
-    assert planes == SUBS and rows == SUBS and slots == LANES and homes % 2 == 0
+    assert planes == SUBS and rows == SUBS and slots == LANES and homes % UNROLL == 0
     vmem = pl.BlockSpec(memory_space=pltpu.VMEM)
     smem = pl.BlockSpec(memory_space=pltpu.SMEM)
 
@@ -344,17 +319,9 @@
         out_shape=jax.ShapeDtypeStruct((bands * homes, 6, slots), jnp.float32),
         in_specs=[smem, vmem, vmem],
         out_specs=vmem,
-        scratch_shapes=[
-            pltpu.VMEM((3 * planes * BINS * SUBS, LANES), jnp.float32),
-            pltpu.VMEM((2, LANES * SUBS + SUBS, LANES), jnp.float32),
-            pltpu.VMEM((2, CELL, LANES, LANES), jnp.float32),
-            pltpu.VMEM(queries, jnp.int32),
-            pltpu.VMEM(queries, jnp.int32),
-            pltpu.VMEM(queries, jnp.int32),
-            pltpu.SMEM(queries, jnp.int32),
-            pltpu.SMEM(queries, jnp.int32),
-            pltpu.SemaphoreType.DMA((2,)),
-        ],
+        scratch_shapes=[pltpu.VMEM((2, LANES * SUBS + SUBS, LANES), jnp.float32)]
+        + [pltpu.VMEM(queries, jnp.int32)] * 4
+        + [pltpu.SMEM(queries, jnp.int32), pltpu.SemaphoreType.DMA],
         compiler_params=pltpu.CompilerParams(vmem_limit_bytes=24 << 20),
     )(me.reshape(1), asked, in_vmem(field))
 

time: 39.3 us -> 37.6 us (0.957)
  Pallas kernels: 12.8 us -> 11.3 us
    pallas_call x1, Pallas kernels: 5.29 us -> 3.83 us  [body(): pl.pallas_call(functools.partial(lookup_kernel, bands=bands, planes=plane...]
  transfers between devices with their start and end apart: 3 -> 3, of which waited for: 1 -> 1; matrix products, arithmetic and copies ran while one was open for 0% -> 0% of each run, Pallas kernels for 13% -> 14%
where the time goes in v4:
time: 37.6 us; the launch traced here: 37.3 us
  blocking collectives  13.3 us (35%)
  Pallas kernels  11.3 us (30%)
  starting transfers between devices  9.87 us (26%)
  waiting for transfers between devices  2.14 us (6%)
  local copies, waits for them, and re-layouts  0.63 us (2%)
    all_to_all x1, blocking collectives, body(): lax.all_to_all(served, ('gx', 'yz'), split_axis=0, concat_axis=0, tiled=T...  13.3 us
    all_to_all x1, starting transfers between devices, body(): lax.all_to_all(asked, ('gx', 'yz'), split_axis=0, concat_axis=0, tiled=True)  7.89 us
    pallas_call x1, Pallas kernels, body(): pl.pallas_call(functools.partial(field_kernel, rows=rows, depth=depth, ch...  5.22 us
    pallas_call x1, Pallas kernels, body(): pl.pallas_call(functools.partial(lookup_kernel, bands=bands, planes=plane...  3.83 us
    pallas_call x1, Pallas kernels, body(): pl.pallas_call(functools.partial(send_kernel, bands=bands, rows=rows), ou...  2.27 us
    all_to_all x1, waiting for transfers between devices, body(): lax.all_to_all(asked, ('gx', 'yz'), split_axis=0, concat_axis=0, tiled=True)  2.13 us
    ppermute x1, starting transfers between devices, body(): next_in = lax.ppermute(next_out, 'yz', swap(1))  1.42 us
  transfers between devices with their start and end apart: 3, of which 1 were waited for; matrix products, arithmetic and copies ran while one was open for 0% of the time, Pallas kernels for 14%

profile of v4, /device:TPU:0, one launch (start us, length us, event | category | flops | bytes accessed | tf_op | source)
XLA Modules:
  0.0 37.3 jit_solution(10394983602590717043)
XLA Ops:
  0.0 2.3 %shard_map.55 = (f32[6,8,2048]{2,1,0:T(8,128)}, f32[6,8,2048]{2,1,0:T(8,128)}, s32[32,3,128]{2,1,0:T(4,128)}, f32[6152,128]{1,0:T(8,128)S(1)}) custom-call(s32[1]{0:T(128)} %bitcast.1.parity, s32[1,8]{1,0:T(1,128)} %bitcast.15, s32[8,128]{1,0:T(8,128)} %bitcast.12, s32[8,128]{1,0:T(8,128)} %bitcast.13, s32[8,128]{1,0:T(8,128)} %bitcast.14, f32[8,8,2048]{2,1,0:T(8,128)} %own_in.3), custom_call_target="tpu_custom_call" | custom-call | tf_op jit(solution)/shard_map/pallas_call | solution.py:261
  2.3 0.6 %collective-permute-start = (f32[6,8,2048]{2,1,0:T(8,128)}, f32[6,8,2048]{2,1,0:T(8,128)}, u32[]{:S(2)}, u32[]{:S(2)}) collective-permute-start(f32[6,8,2048]{2,1,0:T(8,128)} %get-tuple-element.10), channel_id=1, source_target_pairs={{0,1},{1,0},{2,3},{3,2},{4,5},{5,4},{6,7},{7,6},{8,9},{9,8},{10,11... | collective-permute-start | bytes 1179656 | tf_op jit(solution)/shard_map/ppermute | solution.py:292
  2.8 1.4 %collective-permute-start.1 = (f32[6,8,2048]{2,1,0:T(8,128)}, f32[6,8,2048]{2,1,0:T(8,128)}, u32[]{:S(2)}, u32[]{:S(2)}) collective-permute-start(f32[6,8,2048]{2,1,0:T(8,128)} %get-tuple-element.11), channel_id=1, source_target_pairs={{1,2},{2,1},{3,4},{4,3},{5,6},{6,5},{9,10},{10,9},{11,12},{12,11},... | collective-permute-start | bytes 1179656 | tf_op jit(solution)/shard_map/ppermute | solution.py:293
  4.3 7.9 %all-to-all-start = ((s32[32,3,128]{2,1,0:T(4,128)}), s32[32,3,128]{2,1,0:T(4,128)S(1)}, u32[]{:S(2)}, u32[]{:S(2)}) async-start(s32[32,3,128]{2,1,0:T(4,128)} %get-tuple-element.9), calls=%async_computation | async-start | bytes 131072 | tf_op jit(solution)/shard_map/all_to_all | solution.py:294
  12.2 0.0 collective-permute-done.pair_in
  12.2 0.0 collective-permute-done.1.next_in
  12.2 5.2 %shard_map.56.field = f32[6152,128]{1,0:T(8,128)S(1)} custom-call(s32[1]{0:T(128)} %bitcast.1.parity, f32[6,8,2048]{2,1,0:T(8,128)} %collective-permute-done.pair_in, f32[8,8,2048]{2,1,0:T(8,128)} %own_in.3, f32[6,8,2048]{2,1,0:T(8,128)} %collective-permute-done.1.next_in, f32[6152,128]{1,0:T(8,128)S(1)} %get-tuple-element.12.hold), custom_call_target="tpu_custom_call", output_to_operand_aliasing={{}: (4, {})} | custom-call | tf_op jit(solution)/shard_map/pallas_call | solution.py:298
  17.4 2.1 %all-to-all-done.asked = s32[32,3,128]{2,1,0:T(4,128)S(1)} async-done(((s32[32,3,128]{2,1,0:T(4,128)}), s32[32,3,128]{2,1,0:T(4,128)S(1)}, u32[]{:S(2)}, u32[]{:S(2)}) %all-to-all-start) | async-done | bytes 49184 | tf_op jit(solution)/shard_map/all_to_all | solution.py:294
  19.5 3.8 %shard_map.57 = f32[32,6,128]{2,1,0:T(8,128)S(1)} custom-call(s32[1]{0:T(128)} %bitcast.place, s32[32,3,128]{2,1,0:T(4,128)S(1)} %all-to-all-done.asked, f32[6152,128]{1,0:T(8,128)S(1)} %shard_map.56.field), custom_call_target="tpu_custom_call" | custom-call | tf_op jit(solution)/shard_map/pallas_call | solution.py:317
  23.4 13.3 %all_to_all.10 = f32[32,6,128]{2,1,0:T(8,128)S(1)} all-to-all(f32[32,6,128]{2,1,0:T(8,128)S(1)} %shard_map.57), channel_id=1, replica_groups=mesh['gx'=4,'yz'=8] {'gx','yz'}, dimensions={0} | all-to-all | bytes 196608 | tf_op jit(solution)/shard_map/all_to_all | solution.py:328
  36.7 0.6 %copy.7 = f32[6,1,1,1024]{3,2,1,0:T(1,128)} copy(f32[6,1,1,1024]{3,0,2,1:T(8,128)S(1)} %bitcast.11) | data formatting | bytes 49152 | tf_op jit(solution)/shard_map/reshape | solution.py:330
  (1 shorter events, 0.0 us)
Async XLA Ops:
  2.3 9.9 %collective-permute-start = (f32[6,8,2048]{2,1,0:T(8,128)}, f32[6,8,2048]{2,1,0:T(8,128)}, u32[]{:S(2)}, u32[]{:S(2)}) collective-permute-start(f32[6,8,2048]{2,1,0:T(8,128)} %get-tuple-element.10), channel_id=1, source_target_pairs={{0,1},{1,0},{2,3},{3,2},{4,5},{5,4},{6,7},{7,6},{8,9},{9,8},{10,11... | collective-permute-start | bytes 1179656 | tf_op jit(solution)/shard_map/ppermute | solution.py:292
  2.8 9.3 %collective-permute-start.1 = (f32[6,8,2048]{2,1,0:T(8,128)}, f32[6,8,2048]{2,1,0:T(8,128)}, u32[]{:S(2)}, u32[]{:S(2)}) collective-permute-start(f32[6,8,2048]{2,1,0:T(8,128)} %get-tuple-element.11), channel_id=1, source_target_pairs={{1,2},{2,1},{3,4},{4,3},{5,6},{6,5},{9,10},{10,9},{11,12},{12,11},... | collective-permute-start | bytes 1179656 | tf_op jit(solution)/shard_map/ppermute | solution.py:293
  4.3 15.3 %all-to-all-start = ((s32[32,3,128]{2,1,0:T(4,128)}), s32[32,3,128]{2,1,0:T(4,128)S(1)}, u32[]{:S(2)}, u32[]{:S(2)}) async-start(s32[32,3,128]{2,1,0:T(4,128)} %get-tuple-element.9), calls=%async_computation | async-start | bytes 131072 | tf_op jit(solution)/shard_map/all_to_all | solution.py:294

commit v5 on v4

--- a/solution.py
+++ b/solution.py
@@ -44,7 +44,7 @@
     slot = lax.broadcasted_iota(jnp.int32, (1, slots), 1)
     for t in range(tiles):
         cell = jnp.where(slot < counts[0, t], cells[t : t + 1, :], -1)
-        query = jnp.concatenate([cell, zeds[t : t + 1, :], bins[t : t + 1, :]], axis=0)
+        query = jnp.concatenate([cell, zeds[t : t + 1, :] * CELL, bins[t : t + 1, :]], axis=0)
         for band in range(bands):
             asked[band * tiles + t] = query
     moves = [pltpu.make_async_copy(asked, asked_out, gone.at[2, 0])]
@@ -62,33 +62,33 @@
         copy.wait()
 
 
-def field_kernel(parity, pair_in, own_in, next_in, hold, field, before, after, own, mid_01, mid_02, came, *, rows, depth, chunks):
+def field_kernel(parity, pair_in, next_in, pair_out, next_out, hold, field, before, after, own, mid_01, mid_02, came, *, rows, depth, chunks):
     along = taps()
     size = depth // chunks
     per = size // LANES
-    planes = own_in.shape[0]
-
-    def fetches(c, pair_to, next_to):
+
+    kept = rows - HALO
+
+    def fetches(c, is_even):
         zs = pl.ds(c * size, size)
-        return [
-            pltpu.make_async_copy(pair_in.at[:, :, zs], pair_to.at[:, :, zs], came.at[c, 0]),
-            pltpu.make_async_copy(next_in.at[:, :, zs], next_to.at[:, :, zs], came.at[c, 1]),
-        ] + [pltpu.make_async_copy(own_in.at[x, :, zs], own.at[:, x, zs], came.at[c, 2 + x]) for x in range(planes)]
+        low, high = (next_out, pair_out) if is_even else (pair_out, next_out)
+        above, below = (pair_in, next_in) if is_even else (next_in, pair_in)
+        moves = (
+            (below.at[:, :, zs], before.at[:, :, zs]),
+            (low.at[pl.ds(0, kept), :, zs], own.at[pl.ds(0, kept), :, zs]),
+            (high.at[:, :, zs], own.at[pl.ds(kept, HALO), :, zs]),
+            (above.at[:, :, zs], after.at[:, :, zs]),
+        )
+        return [pltpu.make_async_copy(*move, came.at[c, i]) for i, move in enumerate(moves)]
 
     even = parity[0] == 0
-    for c in range(chunks):
-        for copy in fetches(c, after, before)[2:]:
-            copy.start()
-
-        @pl.when(even)
+    for is_even in (True, False):
+
+        @pl.when(even if is_even else jnp.logical_not(even))
         def _():
-            for copy in fetches(c, after, before)[:2]:
-                copy.start()
-
-        @pl.when(jnp.logical_not(even))
-        def _():
-            for copy in fetches(c, before, after)[:2]:
-                copy.start()
+            for c in range(chunks):
+                for copy in fetches(c, is_even):
+                    copy.start()
 
     def along_y(block, _):
         z0 = pl.multiple_of(block * LANES, LANES)
@@ -116,9 +116,9 @@
         return 0
 
     for c in range(chunks):
-        for copy in fetches(c, after, before):
+        for copy in fetches(c, True):
             copy.wait()
-        lax.fori_loop(c * per, (c + 1) * per, along_y, 0, unroll=2)
+        lax.fori_loop(c * per, (c + 1) * per, along_y, 0, unroll=4)
     for buf in (mid_01, mid_02):
         buf[pl.ds(0, SUBS), :] = buf[pl.ds(depth, SUBS), :]
         buf[pl.ds(depth + SUBS, SUBS), :] = buf[pl.ds(SUBS, SUBS), :]
@@ -160,7 +160,7 @@
         step()
 
 
-def lookup_kernel(place, asked, field, out, found, at_v, plane_of, row_of, bin_of, at_s, sent, *, bands, planes, rows):
+def lookup_kernel(place, asked, field, out, found, plane_of, row_of, bin_of, at_s, sent, *, bands, planes, rows):
     me = place[0]
     homes = asked.shape[0] // bands
     first = jnp.maximum(me - 1, 0) * homes
@@ -169,19 +169,19 @@
     scale = np.float32((HALO / 3.0) ** 2)
     subs = lax.broadcasted_iota(jnp.int32, (SUBS, LANES), 0)
 
+    move = pltpu.make_async_copy(asked.at[:, 1, :], at_s, sent)
+    move.start()
+
     def read_rows(i, _):
         for u in range(UNROLL):
             row = first + UNROLL * i + u
-            cell, z, b = asked[row, 0:1, :], asked[row, 1:2, :], asked[row, 2:3, :]
-            at_v[pl.ds(row, 1), :] = z * CELL
+            cell, b = asked[row, 0:1, :], asked[row, 2:3, :]
             plane_of[pl.ds(row, 1), :] = jnp.where(cell >= 0, (row // homes - me) * planes + cell // rows, -planes)
             row_of[pl.ds(row, 1), :] = cell % rows
             bin_of[pl.ds(row, 1), :] = b
         return 0
 
     lax.fori_loop(0, (last - first) // UNROLL, read_rows, 0)
-    move = pltpu.make_async_copy(at_v, at_s, sent)
-    move.start()
 
     def no_row(row, _):
         out[row] = jnp.zeros((6, LANES), jnp.float32)
@@ -261,9 +261,9 @@
     pair_out, next_out, asked, hold = pl.pallas_call(
         functools.partial(send_kernel, bands=bands, rows=rows),
         out_shape=(
-            jax.ShapeDtypeStruct(halo_shape, jnp.float32),
-            jax.ShapeDtypeStruct(halo_shape, jnp.float32),
-            jax.ShapeDtypeStruct((bands * tiles, 3, slots), jnp.int32),
+            pltpu.HBM(halo_shape, jnp.float32),
+            pltpu.HBM(halo_shape, jnp.float32),
+            pltpu.HBM((bands * tiles, 3, slots), jnp.int32),
             pltpu.VMEM(field_shape, jnp.float32),
         ),
         in_specs=[smem] + [hbm] * 5,
@@ -293,24 +293,24 @@
     next_in = lax.ppermute(next_out, "yz", swap(1))
     asked = lax.all_to_all(asked, ("gx", "yz"), split_axis=0, concat_axis=0, tiled=True)
 
-    chunks = 4
+    chunks = 2
     mid_shape = (depth + 2 * SUBS, LANES)
     field = pl.pallas_call(
         functools.partial(field_kernel, rows=rows, depth=depth, chunks=chunks),
         out_shape=pltpu.VMEM(field_shape, jnp.float32),
-        in_specs=[smem, hbm, hbm, hbm, vmem],
+        in_specs=[smem, hbm, hbm, hbm, hbm, vmem],
         out_specs=vmem,
-        input_output_aliases={4: 0},
+        input_output_aliases={5: 0},
         scratch_shapes=[
             pltpu.VMEM(halo_shape, jnp.float32),
             pltpu.VMEM(halo_shape, jnp.float32),
             pltpu.VMEM((rows, planes, depth), jnp.float32),
             pltpu.VMEM(mid_shape, jnp.float32),
             pltpu.VMEM(mid_shape, jnp.float32),
-            pltpu.SemaphoreType.DMA((chunks, 2 + planes)),
+            pltpu.SemaphoreType.DMA((chunks, 4)),
         ],
         compiler_params=pltpu.CompilerParams(vmem_limit_bytes=24 << 20),
-    )(parity, in_hbm(pair_in), in_hbm(potential), in_hbm(next_in), in_vmem(hold))
+    )(parity, in_hbm(pair_in), in_hbm(next_in), in_hbm(pair_out), in_hbm(next_out), in_vmem(hold))
 
     me = lax.axis_index("gx")
     queries = (bands * homes, slots)
@@ -320,10 +320,10 @@
         in_specs=[smem, vmem, vmem],
         out_specs=vmem,
         scratch_shapes=[pltpu.VMEM((2, LANES * SUBS + SUBS, LANES), jnp.float32)]
-        + [pltpu.VMEM(queries, jnp.int32)] * 4
+        + [pltpu.VMEM(queries, jnp.int32)] * 3
         + [pltpu.SMEM(queries, jnp.int32), pltpu.SemaphoreType.DMA],
         compiler_params=pltpu.CompilerParams(vmem_limit_bytes=24 << 20),
-    )(me.reshape(1), asked, in_vmem(field))
+    )(me.reshape(1), in_vmem(asked), in_vmem(field))
 
     returned = lax.all_to_all(served, ("gx", "yz"), split_axis=0, concat_axis=0, tiled=True)
     total = jnp.sum(returned.reshape(bands, tiles, 6, slots), axis=0)

time: 37.6 us -> 36.8 us (0.979)
  Pallas kernels: 11.3 us -> 10.6 us
  blocking collectives: 13.3 us -> 12.6 us
  waiting for transfers between devices: 2.14 us -> 2.73 us
    all_to_all x1, blocking collectives: 13.3 us -> 12.6 us  [body(): lax.all_to_all(served, ('gx', 'yz'), split_axis=0, concat_axis=0, tiled=T...]
    all_to_all x1, waiting for transfers between devices: 2.13 us -> 2.72 us  [body(): lax.all_to_all(asked, ('gx', 'yz'), split_axis=0, concat_axis=0, tiled=True)]
    pallas_call x1, Pallas kernels: 5.22 us -> 4.63 us  [body(): pl.pallas_call(functools.partial(field_kernel, rows=rows, depth=depth, ch...]
  transfers between devices with their start and end apart: 3 -> 3, of which waited for: 1 -> 1; matrix products, arithmetic and copies ran while one was open for 0% -> 0% of each run, Pallas kernels for 14% -> 13%
where the time goes in v5:
time: 36.8 us; the launch traced here: 36.6 us
  blocking collectives  12.6 us (34%)
  Pallas kernels  10.6 us (29%)
  starting transfers between devices  9.87 us (27%)
  waiting for transfers between devices  2.73 us (7%)
  local copies, waits for them, and re-layouts  0.63 us (2%)
    all_to_all x1, blocking collectives, body(): lax.all_to_all(served, ('gx', 'yz'), split_axis=0, concat_axis=0, tiled=T...  12.6 us
    all_to_all x1, starting transfers between devices, body(): lax.all_to_all(asked, ('gx', 'yz'), split_axis=0, concat_axis=0, tiled=True)  7.89 us
    pallas_call x1, Pallas kernels, body(): pl.pallas_call(functools.partial(field_kernel, rows=rows, depth=depth, ch...  4.63 us
    pallas_call x1, Pallas kernels, body(): pl.pallas_call(functools.partial(lookup_kernel, bands=bands, planes=plane...  3.73 us
    all_to_all x1, waiting for transfers between devices, body(): lax.all_to_all(asked, ('gx', 'yz'), split_axis=0, concat_axis=0, tiled=True)  2.72 us
    pallas_call x1, Pallas kernels, body(): pl.pallas_call(functools.partial(send_kernel, bands=bands, rows=rows), ou...  2.27 us
    ppermute x1, starting transfers between devices, body(): next_in = lax.ppermute(next_out, 'yz', swap(1))  1.42 us
  transfers between devices with their start and end apart: 3, of which 1 were waited for; matrix products, arithmetic and copies ran while one was open for 0% of the time, Pallas kernels for 13%

profile of v5, /device:TPU:0, one launch (start us, length us, event | category | flops | bytes accessed | tf_op | source)
XLA Modules:
  0.0 36.6 jit_solution(14806322768947418514)
XLA Ops:
  0.0 2.3 %shard_map.55 = (f32[6,8,2048]{2,1,0:T(8,128)}, f32[6,8,2048]{2,1,0:T(8,128)}, s32[32,3,128]{2,1,0:T(4,128)}, f32[6152,128]{1,0:T(8,128)S(1)}) custom-call(s32[1]{0:T(128)} %bitcast.1.parity, s32[1,8]{1,0:T(1,128)} %bitcast.15, s32[8,128]{1,0:T(8,128)} %bitcast.12, s32[8,128]{1,0:T(8,128)} %bitcast.13, s32[8,128]{1,0:T(8,128)} %bitcast.14, f32[8,8,2048]{2,1,0:T(8,128)} %own_in.1), custom_call_target="tpu_custom_call" | custom-call | tf_op jit(solution)/shard_map/pallas_call | solution.py:261
  2.3 0.6 %collective-permute-start = (f32[6,8,2048]{2,1,0:T(8,128)}, f32[6,8,2048]{2,1,0:T(8,128)}, u32[]{:S(2)}, u32[]{:S(2)}) collective-permute-start(f32[6,8,2048]{2,1,0:T(8,128)} %get-tuple-element.10.pair_out), channel_id=1, source_target_pairs={{0,1},{1,0},{2,3},{3,2},{4,5},{5,4},{6,7},{7,6},{8,9},{9,8},{10,11... | collective-permute-start | bytes 1179656 | tf_op jit(solution)/shard_map/ppermute | solution.py:292
  2.8 1.4 %collective-permute-start.1 = (f32[6,8,2048]{2,1,0:T(8,128)}, f32[6,8,2048]{2,1,0:T(8,128)}, u32[]{:S(2)}, u32[]{:S(2)}) collective-permute-start(f32[6,8,2048]{2,1,0:T(8,128)} %get-tuple-element.11.next_out), channel_id=1, source_target_pairs={{1,2},{2,1},{3,4},{4,3},{5,6},{6,5},{9,10},{10,9},{11,12},{12,11},... | collective-permute-start | bytes 1179656 | tf_op jit(solution)/shard_map/ppermute | solution.py:293
  4.3 7.9 %all-to-all-start = ((s32[32,3,128]{2,1,0:T(4,128)}), s32[32,3,128]{2,1,0:T(4,128)S(1)}, u32[]{:S(2)}, u32[]{:S(2)}) async-start(s32[32,3,128]{2,1,0:T(4,128)} %get-tuple-element.9), calls=%async_computation | async-start | bytes 131072 | tf_op jit(solution)/shard_map/all_to_all | solution.py:294
  12.2 0.0 collective-permute-done.pair_in
  12.2 0.0 collective-permute-done.1.next_in
  12.2 4.6 %shard_map.56.field = f32[6152,128]{1,0:T(8,128)S(1)} custom-call(s32[1]{0:T(128)} %bitcast.1.parity, f32[6,8,2048]{2,1,0:T(8,128)} %collective-permute-done.pair_in, f32[6,8,2048]{2,1,0:T(8,128)} %collective-permute-done.1.next_in, f32[6,8,2048]{2,1,0:T(8,128)} %get-tuple-element.10.pair_out, ...), custom_call_target="tpu_custom_call", output_to_operand_aliasing={{}: (5, {})} | custom-call | tf_op jit(solution)/shard_map/pallas_call | solution.py:298
  16.8 2.7 %all-to-all-done.asked = s32[32,3,128]{2,1,0:T(4,128)S(1)} async-done(((s32[32,3,128]{2,1,0:T(4,128)}), s32[32,3,128]{2,1,0:T(4,128)S(1)}, u32[]{:S(2)}, u32[]{:S(2)}) %all-to-all-start) | async-done | bytes 49184 | tf_op jit(solution)/shard_map/all_to_all | solution.py:294
  19.5 3.7 %shard_map.57 = f32[32,6,128]{2,1,0:T(8,128)S(1)} custom-call(s32[1]{0:T(128)} %bitcast.place, s32[32,3,128]{2,1,0:T(4,128)S(1)} %all-to-all-done.asked, f32[6152,128]{1,0:T(8,128)S(1)} %shard_map.56.field), custom_call_target="tpu_custom_call" | custom-call | tf_op jit(solution)/shard_map/pallas_call | solution.py:317
  23.3 12.6 %all_to_all.10 = f32[32,6,128]{2,1,0:T(8,128)S(1)} all-to-all(f32[32,6,128]{2,1,0:T(8,128)S(1)} %shard_map.57), channel_id=1, replica_groups=mesh['gx'=4,'yz'=8] {'gx','yz'}, dimensions={0} | all-to-all | bytes 196608 | tf_op jit(solution)/shard_map/all_to_all | solution.py:328
  35.9 0.6 %copy.7 = f32[6,1,1,1024]{3,2,1,0:T(1,128)} copy(f32[6,1,1,1024]{3,0,2,1:T(8,128)S(1)} %bitcast.11) | data formatting | bytes 49152 | tf_op jit(solution)/shard_map/reshape | solution.py:330
  (1 shorter events, 0.0 us)
Async XLA Ops:
  2.3 9.9 %collective-permute-start = (f32[6,8,2048]{2,1,0:T(8,128)}, f32[6,8,2048]{2,1,0:T(8,128)}, u32[]{:S(2)}, u32[]{:S(2)}) collective-permute-start(f32[6,8,2048]{2,1,0:T(8,128)} %get-tuple-element.10.pair_out), channel_id=1, source_target_pairs={{0,1},{1,0},{2,3},{3,2},{4,5},{5,4},{6,7},{7,6},{8,9},{9,8},{10,11... | collective-permute-start | bytes 1179656 | tf_op jit(solution)/shard_map/ppermute | solution.py:292
  2.8 9.3 %collective-permute-start.1 = (f32[6,8,2048]{2,1,0:T(8,128)}, f32[6,8,2048]{2,1,0:T(8,128)}, u32[]{:S(2)}, u32[]{:S(2)}) collective-permute-start(f32[6,8,2048]{2,1,0:T(8,128)} %get-tuple-element.11.next_out), channel_id=1, source_target_pairs={{1,2},{2,1},{3,4},{4,3},{5,6},{6,5},{9,10},{10,9},{11,12},{12,11},... | collective-permute-start | bytes 1179656 | tf_op jit(solution)/shard_map/ppermute | solution.py:293
  4.3 15.3 %all-to-all-start = ((s32[32,3,128]{2,1,0:T(4,128)}), s32[32,3,128]{2,1,0:T(4,128)S(1)}, u32[]{:S(2)}, u32[]{:S(2)}) async-start(s32[32,3,128]{2,1,0:T(4,128)} %get-tuple-element.9), calls=%async_computation | async-start | bytes 131072 | tf_op jit(solution)/shard_map/all_to_all | solution.py:294

commit v6 on v5

--- a/solution.py
+++ b/solution.py
@@ -13,6 +13,8 @@
 BINS = 8
 LANES = 128
 SUBS = 8
+EDGES = (1, 4)
+STEPS = 4
 UNROLL = 4
 CELL = 3
 HELD = ((0, 3), (4, 5), (2, 1))
@@ -64,13 +66,13 @@
 
 def field_kernel(parity, pair_in, next_in, pair_out, next_out, hold, field, before, after, own, mid_01, mid_02, came, *, rows, depth, chunks):
     along = taps()
-    size = depth // chunks
-    per = size // LANES
+    per = depth // LANES // STEPS
+    edges = [0] + [per * e for e in EDGES]
 
     kept = rows - HALO
 
     def fetches(c, is_even):
-        zs = pl.ds(c * size, size)
+        zs = pl.ds(edges[c] * LANES, (edges[c + 1] - edges[c]) * LANES)
         low, high = (next_out, pair_out) if is_even else (pair_out, next_out)
         above, below = (pair_in, next_in) if is_even else (next_in, pair_in)
         moves = (
@@ -118,12 +120,12 @@
     for c in range(chunks):
         for copy in fetches(c, True):
             copy.wait()
-        lax.fori_loop(c * per, (c + 1) * per, along_y, 0, unroll=4)
+        lax.fori_loop(edges[c], edges[c + 1], along_y, 0, unroll=4)
     for buf in (mid_01, mid_02):
         buf[pl.ds(0, SUBS), :] = buf[pl.ds(depth, SUBS), :]
         buf[pl.ds(depth + SUBS, SUBS), :] = buf[pl.ds(SUBS, SUBS), :]
 
-    n = 8
+    n = 32
     lower = lax.broadcasted_iota(jnp.int32, (SUBS, LANES), 1) < LANES // 2
     mixed = [jnp.where(lower, along[2][HALO + k], along[0][HALO + k]) for k in range(HALO + 1)]
 
@@ -184,7 +186,7 @@
     lax.fori_loop(0, (last - first) // UNROLL, read_rows, 0)
 
     def no_row(row, _):
-        out[row] = jnp.zeros((6, LANES), jnp.float32)
+        out[row] = jnp.zeros((1, 6 * LANES), jnp.float32)
         return 0
 
     lax.fori_loop(0, first, no_row, 0)
@@ -222,7 +224,7 @@
             w = (bin_of[pl.ds(row, 1), :].astype(jnp.float32) + 0.5) * (1.0 / BINS)
             for a in range(6):
                 value = (1.0 - w) * picked[0, a] + w * picked[1, a]
-                out[row, a, :] = jnp.sum(value * weights[ALONG_X[a]], axis=0)
+                out[row, :, pl.ds(a * LANES, LANES)] = jnp.sum(value * weights[ALONG_X[a]], axis=0, keepdims=True)
 
         return [functools.partial(turn, beyond, c) for c in range(CELL) for beyond in range(2)] + [total]
 
@@ -293,7 +295,7 @@
     next_in = lax.ppermute(next_out, "yz", swap(1))
     asked = lax.all_to_all(asked, ("gx", "yz"), split_axis=0, concat_axis=0, tiled=True)
 
-    chunks = 2
+    chunks = len(EDGES)
     mid_shape = (depth + 2 * SUBS, LANES)
     field = pl.pallas_call(
         functools.partial(field_kernel, rows=rows, depth=depth, chunks=chunks),
@@ -316,7 +318,7 @@
     queries = (bands * homes, slots)
     served = pl.pallas_call(
         functools.partial(lookup_kernel, bands=bands, planes=planes, rows=rows),
-        out_shape=jax.ShapeDtypeStruct((bands * homes, 6, slots), jnp.float32),
+        out_shape=jax.ShapeDtypeStruct((bands * homes, 1, 6 * slots), jnp.float32),
         in_specs=[smem, vmem, vmem],
         out_specs=vmem,
         scratch_shapes=[pltpu.VMEM((2, LANES * SUBS + SUBS, LANES), jnp.float32)]

time: 36.8 us -> 36.1 us (0.981)
  local copies, waits for them, and re-layouts: 0.63 us -> 0 us
  other arithmetic: 0.01 us -> 0.61 us
  blocking collectives: 12.6 us -> 12 us
    all_to_all x1, blocking collectives: 12.6 us -> 12 us  [body(): lax.all_to_all(served, ('gx', 'yz'), split_axis=0, concat_axis=0, tiled=T...]
    reshape x1 -> x0, local copies, waits for them, and re-layouts: 0.63 us -> none  [body(): return total.transpose(1, 0, 2).reshape(6, 1, 1, tiles * slots)]
    reduce_sum x1, other arithmetic: 0.01 us -> 0.61 us  [body(): total = jnp.sum(returned.reshape(bands, tiles, 6, slots), axis=0)]
  transfers between devices with their start and end apart: 3 -> 3, of which waited for: 1 -> 1; matrix products, arithmetic and copies ran while one was open for 0% -> 0% of each run, Pallas kernels for 13% -> 12%
where the time goes in v6:
time: 36.1 us; the launch traced here: 35.8 us
  blocking collectives  12 us (33%)
  Pallas kernels  10.3 us (29%)
  starting transfers between devices  9.87 us (27%)
  waiting for transfers between devices  3 us (8%)
  other arithmetic  0.61 us (2%)
    all_to_all x1, blocking collectives, body(): lax.all_to_all(served, ('gx', 'yz'), split_axis=0, concat_axis=0, tiled=T...  12 us
    all_to_all x1, starting transfers between devices, body(): lax.all_to_all(asked, ('gx', 'yz'), split_axis=0, concat_axis=0, tiled=True)  7.89 us
    pallas_call x1, Pallas kernels, body(): pl.pallas_call(functools.partial(field_kernel, rows=rows, depth=depth, ch...  4.36 us
    pallas_call x1, Pallas kernels, body(): pl.pallas_call(functools.partial(lookup_kernel, bands=bands, planes=plane...  3.71 us
    all_to_all x1, waiting for transfers between devices, body(): lax.all_to_all(asked, ('gx', 'yz'), split_axis=0, concat_axis=0, tiled=True)  3 us
    pallas_call x1, Pallas kernels, body(): pl.pallas_call(functools.partial(send_kernel, bands=bands, rows=rows), ou...  2.27 us
    ppermute x1, starting transfers between devices, body(): next_in = lax.ppermute(next_out, 'yz', swap(1))  1.42 us
  transfers between devices with their start and end apart: 3, of which 1 were waited for; matrix products, arithmetic and copies ran while one was open for 0% of the time, Pallas kernels for 12%

profile of v6, /device:TPU:0, one launch (start us, length us, event | category | flops | bytes accessed | tf_op | source)
XLA Modules:
  0.0 35.8 jit_solution(5748005940918163247)
XLA Ops:
  0.0 2.3 %shard_map.55 = (f32[6,8,2048]{2,1,0:T(8,128)}, f32[6,8,2048]{2,1,0:T(8,128)}, s32[32,3,128]{2,1,0:T(4,128)}, f32[6152,128]{1,0:T(8,128)S(1)}) custom-call(s32[1]{0:T(128)} %bitcast.1.parity, s32[1,8]{1,0:T(1,128)} %bitcast.14, s32[8,128]{1,0:T(8,128)} %bitcast.11, s32[8,128]{1,0:T(8,128)} %bitcast.12, s32[8,128]{1,0:T(8,128)} %bitcast.13, f32[8,8,2048]{2,1,0:T(8,128)} %own_in.1), custom_call_target="tpu_custom_call" | custom-call | tf_op jit(solution)/shard_map/pallas_call | solution.py:263
  2.3 0.6 %collective-permute-start = (f32[6,8,2048]{2,1,0:T(8,128)}, f32[6,8,2048]{2,1,0:T(8,128)}, u32[]{:S(2)}, u32[]{:S(2)}) collective-permute-start(f32[6,8,2048]{2,1,0:T(8,128)} %get-tuple-element.10.pair_out), channel_id=1, source_target_pairs={{0,1},{1,0},{2,3},{3,2},{4,5},{5,4},{6,7},{7,6},{8,9},{9,8},{10,11... | collective-permute-start | bytes 1179656 | tf_op jit(solution)/shard_map/ppermute | solution.py:294
  2.8 1.4 %collective-permute-start.1 = (f32[6,8,2048]{2,1,0:T(8,128)}, f32[6,8,2048]{2,1,0:T(8,128)}, u32[]{:S(2)}, u32[]{:S(2)}) collective-permute-start(f32[6,8,2048]{2,1,0:T(8,128)} %get-tuple-element.11.next_out), channel_id=1, source_target_pairs={{1,2},{2,1},{3,4},{4,3},{5,6},{6,5},{9,10},{10,9},{11,12},{12,11},... | collective-permute-start | bytes 1179656 | tf_op jit(solution)/shard_map/ppermute | solution.py:295
  4.3 7.9 %all-to-all-start = ((s32[32,3,128]{2,1,0:T(4,128)}), s32[32,3,128]{2,1,0:T(4,128)S(1)}, u32[]{:S(2)}, u32[]{:S(2)}) async-start(s32[32,3,128]{2,1,0:T(4,128)} %get-tuple-element.9), calls=%async_computation | async-start | bytes 131072 | tf_op jit(solution)/shard_map/all_to_all | solution.py:296
  12.2 0.0 collective-permute-done.pair_in
  12.2 0.0 collective-permute-done.1.next_in
  12.2 4.4 %shard_map.56.field = f32[6152,128]{1,0:T(8,128)S(1)} custom-call(s32[1]{0:T(128)} %bitcast.1.parity, f32[6,8,2048]{2,1,0:T(8,128)} %collective-permute-done.pair_in, f32[6,8,2048]{2,1,0:T(8,128)} %collective-permute-done.1.next_in, f32[6,8,2048]{2,1,0:T(8,128)} %get-tuple-element.10.pair_out, ...), custom_call_target="tpu_custom_call", output_to_operand_aliasing={{}: (5, {})} | custom-call | tf_op jit(solution)/shard_map/pallas_call | solution.py:300
  16.5 3.0 %all-to-all-done.asked = s32[32,3,128]{2,1,0:T(4,128)S(1)} async-done(((s32[32,3,128]{2,1,0:T(4,128)}), s32[32,3,128]{2,1,0:T(4,128)S(1)}, u32[]{:S(2)}, u32[]{:S(2)}) %all-to-all-start) | async-done | bytes 49184 | tf_op jit(solution)/shard_map/all_to_all | solution.py:296
  19.5 3.7 %shard_map.57 = f32[32,1,768]{2,1,0:T(1,128)S(1)} custom-call(s32[1]{0:T(128)} %bitcast.place, s32[32,3,128]{2,1,0:T(4,128)S(1)} %all-to-all-done.asked, f32[6152,128]{1,0:T(8,128)S(1)} %shard_map.56.field), custom_call_target="tpu_custom_call" | custom-call | tf_op jit(solution)/shard_map/pallas_call | solution.py:319
  23.3 12.0 %all_to_all.10 = f32[32,1,768]{2,1,0:T(1,128)S(1)} all-to-all(f32[32,1,768]{2,1,0:T(1,128)S(1)} %shard_map.57), channel_id=1, replica_groups=mesh['gx'=4,'yz'=8] {'gx','yz'}, dimensions={0} | all-to-all | bytes 196608 | tf_op jit(solution)/shard_map/all_to_all | solution.py:330
  35.2 0.6 %bitcast_reduce_fusion = f32[8,6,128]{2,0,1:T(8,128)} fusion(f32[32,1,768]{2,1,0:T(1,128)S(1)} %all_to_all.10), kind=kLoop, calls=%fused_computation | loop fusion | flops 18432 | bytes 122880 | tf_op jit(solution)/shard_map/reduce_sum | solution.py:331
Async XLA Ops:
  2.3 9.9 %collective-permute-start = (f32[6,8,2048]{2,1,0:T(8,128)}, f32[6,8,2048]{2,1,0:T(8,128)}, u32[]{:S(2)}, u32[]{:S(2)}) collective-permute-start(f32[6,8,2048]{2,1,0:T(8,128)} %get-tuple-element.10.pair_out), channel_id=1, source_target_pairs={{0,1},{1,0},{2,3},{3,2},{4,5},{5,4},{6,7},{7,6},{8,9},{9,8},{10,11... | collective-permute-start | bytes 1179656 | tf_op jit(solution)/shard_map/ppermute | solution.py:294
  2.8 9.3 %collective-permute-start.1 = (f32[6,8,2048]{2,1,0:T(8,128)}, f32[6,8,2048]{2,1,0:T(8,128)}, u32[]{:S(2)}, u32[]{:S(2)}) collective-permute-start(f32[6,8,2048]{2,1,0:T(8,128)} %get-tuple-element.11.next_out), channel_id=1, source_target_pairs={{1,2},{2,1},{3,4},{4,3},{5,6},{6,5},{9,10},{10,9},{11,12},{12,11},... | collective-permute-start | bytes 1179656 | tf_op jit(solution)/shard_map/ppermute | solution.py:295
  4.3 15.3 %all-to-all-start = ((s32[32,3,128]{2,1,0:T(4,128)}), s32[32,3,128]{2,1,0:T(4,128)S(1)}, u32[]{:S(2)}, u32[]{:S(2)}) async-start(s32[32,3,128]{2,1,0:T(4,128)} %get-tuple-element.9), calls=%async_computation | async-start | bytes 131072 | tf_op jit(solution)/shard_map/all_to_all | solution.py:296
